TPU v7x, 32 devices: a whole 2x2x4 slice. The times are simulated.
32 devices in a mesh: tok: 8 (over z, y), grp: 4 (over x, core).
Axes of the slice: x: 2, y: 2, z: 4, core: 2. Of those that a mesh axis runs over, the one named last changes fastest.
Arguments:
- tokens: bfloat16 [4, 8192, 768], P('grp', 'tok'), may hold values from -6 to 6
- upstream: bfloat16 [4, 8192, 768], P('grp', 'tok'), may hold values from -6 to 6
- cluster_pos: int32 [4, 12, 8192], P('grp', None, 'tok'), may hold values from 0 to 8191, as said below
- project_in: bfloat16 [768, 2304], P(('tok', 'grp')), may hold values from -0.21875 to 0.21875
- query_bias: bfloat16 [768], P(('tok', 'grp')), may hold values from -3 to 3
- value_bias: bfloat16 [768], P(('tok', 'grp')), may hold values from -3 to 3
- project_out: bfloat16 [768, 768], P(('tok', 'grp')), may hold values from -1.25 to 1.25
- output_bias: bfloat16 [768], P(('tok', 'grp')), may hold values from -2 to 2
- first_gain: bfloat16 [768], P(('tok', 'grp')), may hold values from 0.5 to 1.5
- first_shift: bfloat16 [768], P(('tok', 'grp')), may hold values from -2 to 2
- expand: bfloat16 [768, 3072], P(('tok', 'grp')), may hold values from -0.21875 to 0.21875
- expand_bias: bfloat16 [3072], P(('tok', 'grp')), may hold values from -2 to 2
- contract: bfloat16 [3072, 768], P(('tok', 'grp')), may hold values from -0.109375 to 0.109375
- contract_bias: bfloat16 [768], P(('tok', 'grp')), may hold values from -2 to 2
- second_gain: bfloat16 [768], P(('tok', 'grp')), may hold values from 0.5 to 1.5
- second_shift: bfloat16 [768], P(('tok', 'grp')), may hold values from -2 to 2
Outputs:
- activations: bfloat16 [4, 8192, 768], P('grp', 'tok')
- token_grad: float32 [4, 8192, 768], P('grp', 'tok')
- project_in_grad: float32 [768, 2304], P(('tok', 'grp'))
- query_bias_grad: float32 [768], P(('tok', 'grp'))
- value_bias_grad: float32 [768], P(('tok', 'grp'))
- project_out_grad: float32 [768, 768], P(('tok', 'grp'))
- output_bias_grad: float32 [768], P(('tok', 'grp'))
- first_gain_grad: float32 [768], P(('tok', 'grp'))
- first_shift_grad: float32 [768], P(('tok', 'grp'))
- expand_grad: float32 [768, 3072], P(('tok', 'grp'))
- expand_bias_grad: float32 [3072], P(('tok', 'grp'))
- contract_grad: float32 [3072, 768], P(('tok', 'grp'))
- contract_bias_grad: float32 [768], P(('tok', 'grp'))
- second_gain_grad: float32 [768], P(('tok', 'grp'))
- second_shift_grad: float32 [768], P(('tok', 'grp'))
Inputs may be any that keep to these rules, and one draw needn't show every extreme that they name: `cluster_pos`: positions of one group and head form a permutation of the group's rows that maps each aligned block of 4096 rows onto itself. A block is either one sequence of 4096 tokens, in which every device of the block sends exactly 256 of its rows to every device of the block, itself included, or 8 sequences of 512 tokens, each permuted within itself. Each group has 2 blocks; on this slice both are of the first kind. Every cluster holds tokens of one sequence.
All inputs are finite; a program needn't handle non-finite values.
Results may differ from a plain program's by a relative error of at most 0.013.
Values may be sent and summed in bfloat16 or wider, within the bound.
A program may use at most 192 MiB of HBM per device.

v0:
```python
import jax
import jax.numpy as jnp
from jax import lax
from jax.sharding import PartitionSpec as P

CL = 128
LONG = 4096


epsilon = 1e-05
root_half = 0.7071067811865476
density_norm = 0.3989422804014327


def swapped(block, axis, stride):
    count = lax.axis_size(axis)
    route = []
    for low in range(count):
        high = low | 1 << stride
        if high != low and high < count:
            route += [(low, high), (high, low)]
    return lax.ppermute(block, axis, route)


def normalize(hidden, gain, shift):
    centred = hidden - jnp.mean(hidden, axis=1, keepdims=True)
    inverse_std = lax.rsqrt(jnp.mean(centred * centred, axis=1, keepdims=True) + epsilon)
    unit = centred * inverse_std
    return (unit * gain + shift, unit, inverse_std)


def normalize_back(grad_out, gain, unit, inverse_std):
    scaled = grad_out * gain
    return inverse_std * (
        scaled
        - jnp.mean(scaled, axis=1, keepdims=True)
        - unit * jnp.mean(scaled * unit, axis=1, keepdims=True)
    )


def sectioned(parts, span, mover):
    for level in range(span.bit_length() - 1):
        shaped = tuple(
            (piece.reshape((span >> level + 1, 2, 1 << level) + piece.shape[1:]) for piece in parts)
        )
        moved = mover(tuple((piece[:, 1] for piece in shaped)), level)
        parts = tuple(
            (
                piece.at[:, 1].set(fresh).reshape((span,) + piece.shape[3:])
                for piece, fresh in zip(shaped, moved)
            )
        )
    return parts


def pack(values, send_slot, rank, span, share):
    heads, count, width = values.shape
    lanes = jnp.arange(heads, dtype=jnp.int32)[:, None]
    buffer = (
        jnp.zeros((span, heads, share, width), values.dtype)
        .at[send_slot, lanes, rank]
        .set(values, mode="drop")
    )
    return buffer.reshape(span, heads, share * width)


def pack_index(own_at, send_slot, rank, span, share):
    heads, count = own_at.shape
    lanes = jnp.arange(heads, dtype=jnp.int32)[:, None]
    return (
        jnp.full((span, heads, share), count, jnp.int32)
        .at[send_slot, lanes, rank]
        .set(own_at, mode="drop")
    )


def settle(arrived, arrived_at, values, local_at):
    heads, count, width = values.shape
    span = arrived.shape[0]
    lanes = jnp.arange(heads, dtype=jnp.int32)
    result = jnp.zeros_like(values).at[lanes[:, None], local_at].set(values, mode="drop")
    return result.at[lanes[None, :, None], arrived_at].set(
        arrived.reshape(span, heads, -1, width), mode="drop"
    )


def collect(values, arrived_at):
    heads, count, width = values.shape
    span = arrived_at.shape[0]
    lanes = jnp.arange(heads, dtype=jnp.int32)[None, :, None]
    taken = values[lanes, jnp.minimum(arrived_at, count - 1)]
    return taken.reshape(span, heads, -1)


def restore(returned, send_slot, rank, values, own_at, remote):
    heads, count, width = values.shape
    span = returned.shape[0]
    share = returned.shape[2] // width
    lanes = jnp.arange(heads, dtype=jnp.int32)[:, None]
    shaped = returned.reshape(span, heads, share, width)
    far_rows = shaped[jnp.minimum(send_slot, span - 1), lanes, jnp.clip(rank, 0, share - 1)]
    near_rows = values[lanes, own_at]
    return jnp.where(remote[:, :, None], far_rows, near_rows)


def shards(
    tokens,
    upstream,
    cluster_pos,
    project_in,
    query_bias,
    value_bias,
    project_out,
    output_bias,
    first_gain,
    first_shift,
    expand,
    expand_bias,
    contract,
    contract_bias,
    second_gain,
    second_shift,
):
    (
        project_in,
        query_bias,
        value_bias,
        project_out,
        output_bias,
        first_gain,
        first_shift,
        expand,
        expand_bias,
        contract,
        contract_bias,
        second_gain,
        second_shift,
    ) = (
        lax.all_gather(project_in, ("tok", "grp"), axis=0, tiled=True),
        lax.all_gather(query_bias, ("tok", "grp"), axis=0, tiled=True),
        lax.all_gather(value_bias, ("tok", "grp"), axis=0, tiled=True),
        lax.all_gather(project_out, ("tok", "grp"), axis=0, tiled=True),
        lax.all_gather(output_bias, ("tok", "grp"), axis=0, tiled=True),
        lax.all_gather(first_gain, ("tok", "grp"), axis=0, tiled=True),
        lax.all_gather(first_shift, ("tok", "grp"), axis=0, tiled=True),
        lax.all_gather(expand, ("tok", "grp"), axis=0, tiled=True),
        lax.all_gather(expand_bias, ("tok", "grp"), axis=0, tiled=True),
        lax.all_gather(contract, ("tok", "grp"), axis=0, tiled=True),
        lax.all_gather(contract_bias, ("tok", "grp"), axis=0, tiled=True),
        lax.all_gather(second_gain, ("tok", "grp"), axis=0, tiled=True),
        lax.all_gather(second_shift, ("tok", "grp"), axis=0, tiled=True),
    )
    floats = jnp.float32
    halves = jnp.bfloat16
    inputs = tokens[0]
    count, width = inputs.shape
    positions = cluster_pos[0]
    heads = positions.shape[0]
    head_dim = width // heads
    span = LONG // count
    share = count // span
    scale = head_dim ** (-0.5)
    offset = lax.axis_index("tok") % span
    slot = jnp.bitwise_xor(positions // count % span, offset)
    remote = slot != 0
    marks = (slot[:, :, None] == jnp.arange(span, dtype=jnp.int32)).astype(jnp.int32)
    rank = jnp.sum(jnp.cumsum(marks, axis=1) * marks, axis=2) - 1
    send_slot = jnp.where(remote, slot, span)
    own_at = positions % count
    local_at = jnp.where(remote, count, own_at)
    bias_all = jnp.concatenate(
        [query_bias.astype(floats), jnp.zeros((width,), floats), value_bias.astype(floats)]
    )
    joined = (jnp.dot(inputs, project_in, preferred_element_type=floats) + bias_all).astype(halves)
    per_head = (
        joined.reshape(count, 3, heads, head_dim)
        .transpose(2, 0, 1, 3)
        .reshape(heads, count, 3 * head_dim)
    )
    outgoing = pack(per_head, send_slot, rank, span, share)
    outgoing_at = pack_index(own_at, send_slot, rank, span, share)
    arrived, arrived_at = sectioned(
        (outgoing, outgoing_at),
        span,
        lambda pieces, level: swapped((pieces[0], pieces[1]), "tok", level),
    )
    clustered = settle(arrived, arrived_at, per_head, local_at)
    grouped = clustered.reshape(heads, count // CL, CL, 3 * head_dim)
    query = grouped[..., :head_dim]
    keys = grouped[..., head_dim : 2 * head_dim]
    values = grouped[..., 2 * head_dim :]
    scores = jnp.einsum("hcqd,hckd->hcqk", query, keys, preferred_element_type=floats) * scale
    summit = jnp.max(scores, axis=3, keepdims=True)
    log_total = summit + jnp.log(jnp.sum(jnp.exp(scores - summit), axis=3, keepdims=True))
    probs_first = jnp.exp(scores - log_total)
    probs_low = probs_first.astype(halves)
    attended = (
        jnp.einsum("hcqk,hckd->hcqd", probs_low, values, preferred_element_type=floats)
        .astype(halves)
        .reshape(heads, count, head_dim)
    )
    returning = collect(attended, arrived_at)
    came_back = sectioned(
        (returning,), span, lambda pieces, level: (swapped(pieces[0], "tok", level),)
    )[0]
    head_rows = restore(came_back, send_slot, rank, attended, own_at, remote)
    merged = head_rows.transpose(1, 0, 2).reshape(count, width)
    branch = jnp.dot(merged, project_out, preferred_element_type=floats) + output_bias.astype(
        floats
    )
    gain_one = first_gain.astype(floats)
    gain_two = second_gain.astype(floats)
    normed_one, unit_one, inverse_one = normalize(
        inputs.astype(floats) + branch, gain_one, first_shift.astype(floats)
    )
    normed_low = normed_one.astype(halves)
    inner = jnp.dot(normed_low, expand, preferred_element_type=floats) + expand_bias.astype(floats)
    lifted = jax.nn.gelu(inner, approximate=False).astype(halves)
    second_sum = (
        normed_one
        + jnp.dot(lifted, contract, preferred_element_type=floats)
        + contract_bias.astype(floats)
    )
    result, unit_two, inverse_two = normalize(second_sum, gain_two, second_shift.astype(floats))
    cotangent = upstream[0].astype(floats)
    second_gain_grad = jnp.sum(cotangent * unit_two, axis=0)
    second_shift_grad = jnp.sum(cotangent, axis=0)
    grad_second = normalize_back(cotangent, gain_two, unit_two, inverse_two)
    grad_mid = grad_second.astype(halves)
    contract_bias_grad = jnp.sum(grad_mid.astype(floats), axis=0)
    contract_grad = jnp.einsum("rf,rd->fd", lifted, grad_mid, preferred_element_type=floats)
    grad_lifted = jnp.einsum("rd,fd->rf", grad_mid, contract, preferred_element_type=floats)
    slope = (
        0.5 * (1.0 + lax.erf(inner * root_half))
        + inner * jnp.exp(-0.5 * inner * inner) * density_norm
    )
    grad_inner = (grad_lifted * slope).astype(halves)
    expand_bias_grad = jnp.sum(grad_inner.astype(floats), axis=0)
    expand_grad = jnp.einsum("rd,rf->df", normed_low, grad_inner, preferred_element_type=floats)
    grad_normed = grad_second + jnp.einsum(
        "rf,df->rd", grad_inner, expand, preferred_element_type=floats
    )
    first_gain_grad = jnp.sum(grad_normed * unit_one, axis=0)
    first_shift_grad = jnp.sum(grad_normed, axis=0)
    grad_first = normalize_back(grad_normed, gain_one, unit_one, inverse_one)
    grad_branch = grad_first.astype(halves)
    output_bias_grad = jnp.sum(grad_branch.astype(floats), axis=0)
    project_out_grad = jnp.einsum("rd,re->de", merged, grad_branch, preferred_element_type=floats)
    grad_merged = jnp.einsum(
        "re,de->rd", grad_branch, project_out, preferred_element_type=floats
    ).astype(halves)
    grad_heads = grad_merged.reshape(count, heads, head_dim).transpose(1, 0, 2)
    sending = pack(grad_heads, send_slot, rank, span, share)
    delivered = sectioned(
        (sending,), span, lambda pieces, level: (swapped(pieces[0], "tok", level),)
    )[0]
    grad_attended = settle(delivered, arrived_at, grad_heads, local_at).reshape(
        heads, count // CL, CL, head_dim
    )
    again = jnp.einsum("hcqd,hckd->hcqk", query, keys, preferred_element_type=floats) * scale
    probs = jnp.exp(again - log_total)
    probs_again = probs.astype(halves)
    grad_probs = jnp.einsum("hcqd,hckd->hcqk", grad_attended, values, preferred_element_type=floats)
    row_dot = jnp.sum(grad_probs * probs, axis=3, keepdims=True)
    grad_scores = (probs * (grad_probs - row_dot)).astype(halves)
    grad_query = (
        jnp.einsum("hcqk,hckd->hcqd", grad_scores, keys, preferred_element_type=floats) * scale
    )
    grad_keys = (
        jnp.einsum("hcqk,hcqd->hckd", grad_scores, query, preferred_element_type=floats) * scale
    )
    grad_values = jnp.einsum(
        "hcqk,hcqd->hckd", probs_again, grad_attended, preferred_element_type=floats
    )
    grad_grouped = jnp.concatenate([grad_query, grad_keys, grad_values], axis=3).astype(halves)
    grad_ordered = grad_grouped.reshape(heads, count, 3 * head_dim)
    leaving = collect(grad_ordered, arrived_at)
    brought = sectioned(
        (leaving,), span, lambda pieces, level: (swapped(pieces[0], "tok", level),)
    )[0]
    grad_rows = restore(brought, send_slot, rank, grad_ordered, own_at, remote)
    grad_joined = (
        grad_rows.reshape(heads, count, 3, head_dim).transpose(1, 2, 0, 3).reshape(count, 3 * width)
    )
    column_sums = jnp.sum(grad_joined.astype(floats), axis=0)
    query_bias_grad = column_sums[:width]
    value_bias_grad = column_sums[2 * width :]
    project_in_grad = jnp.einsum("rd,re->de", inputs, grad_joined, preferred_element_type=floats)
    token_grad = grad_first + jnp.einsum(
        "re,de->rd", grad_joined, project_in, preferred_element_type=floats
    )
    (
        project_in_grad,
        query_bias_grad,
        value_bias_grad,
        project_out_grad,
        output_bias_grad,
        first_gain_grad,
        first_shift_grad,
        expand_grad,
        expand_bias_grad,
        contract_grad,
        contract_bias_grad,
        second_gain_grad,
        second_shift_grad,
    ) = (
        lax.psum_scatter(project_in_grad, ("tok", "grp"), scatter_dimension=0, tiled=True),
        lax.psum_scatter(query_bias_grad, ("tok", "grp"), scatter_dimension=0, tiled=True),
        lax.psum_scatter(value_bias_grad, ("tok", "grp"), scatter_dimension=0, tiled=True),
        lax.psum_scatter(project_out_grad, ("tok", "grp"), scatter_dimension=0, tiled=True),
        lax.psum_scatter(output_bias_grad, ("tok", "grp"), scatter_dimension=0, tiled=True),
        lax.psum_scatter(first_gain_grad, ("tok", "grp"), scatter_dimension=0, tiled=True),
        lax.psum_scatter(first_shift_grad, ("tok", "grp"), scatter_dimension=0, tiled=True),
        lax.psum_scatter(expand_grad, ("tok", "grp"), scatter_dimension=0, tiled=True),
        lax.psum_scatter(expand_bias_grad, ("tok", "grp"), scatter_dimension=0, tiled=True),
        lax.psum_scatter(contract_grad, ("tok", "grp"), scatter_dimension=0, tiled=True),
        lax.psum_scatter(contract_bias_grad, ("tok", "grp"), scatter_dimension=0, tiled=True),
        lax.psum_scatter(second_gain_grad, ("tok", "grp"), scatter_dimension=0, tiled=True),
        lax.psum_scatter(second_shift_grad, ("tok", "grp"), scatter_dimension=0, tiled=True),
    )
    return (
        result.astype(halves)[None],
        token_grad[None],
        project_in_grad,
        query_bias_grad,
        value_bias_grad,
        project_out_grad,
        output_bias_grad,
        first_gain_grad,
        first_shift_grad,
        expand_grad,
        expand_bias_grad,
        contract_grad,
        contract_bias_grad,
        second_gain_grad,
        second_shift_grad,
    )


def solution(mesh):
    placed = (
        P("grp", "tok", None),
        P("grp", "tok", None),
        P("grp", None, "tok"),
        P(("tok", "grp"), None),
        P(("tok", "grp")),
        P(("tok", "grp")),
        P(("tok", "grp"), None),
        P(("tok", "grp")),
        P(("tok", "grp")),
        P(("tok", "grp")),
        P(("tok", "grp"), None),
        P(("tok", "grp")),
        P(("tok", "grp"), None),
        P(("tok", "grp")),
        P(("tok", "grp")),
        P(("tok", "grp")),
    )
    return jax.shard_map(
        shards,
        mesh=mesh,
        in_specs=placed,
        out_specs=(
            P("grp", "tok", None),
            P("grp", "tok", None),
            P(("tok", "grp"), None),
            P(("tok", "grp")),
            P(("tok", "grp")),
            P(("tok", "grp"), None),
            P(("tok", "grp")),
            P(("tok", "grp")),
            P(("tok", "grp")),
            P(("tok", "grp"), None),
            P(("tok", "grp")),
            P(("tok", "grp"), None),
            P(("tok", "grp")),
            P(("tok", "grp")),
            P(("tok", "grp")),
        ),
        check_vma=False,
    )
```

profile of v0, /device:TPU:0, one launch (start us, length us, event | category | flops | bytes accessed | tf_op | source)
XLA Modules:
  0.0 2190.2 jit_solution(6454550354077643893)
XLA Ops:
  8.9 13.5 reduce-window.6
  35.7 43.0 %all-reduce.19 = (bf16[768]{0:T(1024)(128)(2,1)S(1)}, bf16[768]{0:T(1024)(128)(2,1)S(1)}, bf16[768]{0:T(1024)(128)(2,1)S(1)}, bf16[768]{0:T(1024)(128)(2,1)S(1)}...) all-reduce(bf16[768]{0:T(1024)(128)(2,1)S(1)} %dynamic-update-slice, ...), channel_id=1, replica_groups=mesh['tok'=8,'grp'=4] {'tok','grp'}, use_global_device_ids=true, to_apply=%add.1 | all-reduce | flops 9216 | bytes 36864
  92.8 18.3 copy.239
  111.1 23.2 %reshape.1045 = bf16[12288,192]{1,0:T(8,128)(2,1)} reshape(bf16[12,1024,3,64]{3,2,1,0:T(4,128)(2,1)} %copy.239) | data formatting | bytes 9437184 | tf_op jit(solution)/shard_map/reshape | solution.py:178
  134.3 56.3 %scatter_custom_fusion.2 = bf16[12288,192]{1,0:T(8,128)(2,1)} fusion(s32[12288]{0:T(1024)S(1)} %reshape.983, bf16[12288,192]{1,0:T(8,128)(2,1)} %reshape.1045, bf16[]{:T(256)} %constant.338.clone.1), kind=kCustom, calls=%fused_computation.70 | custom fusion | bytes 4719104
  218.3 42.4 %collective-permute-done.2 = bf16[2,1,12,49152]{3,0,2,1:T(2,128)(2,1)} collective-permute-done((bf16[2,1,12,49152]{3,0,2,1:T(2,128)(2,1)S(1)}, bf16[2,1,12,49152]{3,0,2,1:T(2,128)(2,1)}, u32[]{:S(2)}, u32[]{:S(2)}) %collective-permute-start.2) | collective-permute-done | bytes 2359328 | tf_op jit(solution)/shard_map/ppermute | solution.py:22
  273.0 45.4 %scatter_custom_fusion.1 = s32[12288]{0:T(1024)S(1)} fusion(s32[12288]{0:T(1024)S(1)} %reshape.977, s32[12288]{0:T(1024)S(1)} %reshape.979, s32[]{:T(128)} %constant.339.clone.1), kind=kCustom, calls=%fused_computation.214 | custom fusion | bytes 49156
  327.1 56.3 %scatter_custom_fusion = bf16[12288,192]{1,0:T(8,128)(2,1)} fusion(s32[12288]{0:T(1024)S(1)} %reshape.971, bf16[12288,192]{1,0:T(8,128)(2,1)} %reshape.1045, bf16[]{:T(256)} %constant.338.clone.1), kind=kCustom, calls=%fused_computation.72 | custom fusion | bytes 4719104
  396.5 59.3 %scatter_fusion = bf16[12288,192]{1,0:T(8,128)(2,1)} fusion(bf16[12288,192]{1,0:T(8,128)(2,1)} %scatter_custom_fusion, s32[12288]{0:T(1024)S(1)} %reshape.989, bf16[12288,192]{1,0:T(8,128)(2,1)} %reshape.991), kind=kCustom, calls=%fused_computation.9 | custom fusion | bytes 14204928
  470.1 120.6 %gather_fusion = bf16[12288,64]{1,0:T(8,128)(2,1)} fusion(bf16[12,1024,64]{2,1,0:T(8,128)(2,1)S(1)} %bitcast.205, s32[12288]{0:T(1024)S(1)} %bitcast.203), kind=kCustom, calls=%fused_computation | custom fusion | bytes 3244032 | tf_op jit(solution)/shard_map/gather | solution.py:91
  626.4 120.6 %gather_fusion.2 = bf16[12288,64]{1,0:T(8,128)(2,1)} fusion(bf16[12,1024,64]{2,1,0:T(8,128)(2,1)S(1)} %bitcast.206, s32[12288]{0:T(1024)S(1)} %bitcast.201), kind=kCustom, calls=%fused_computation.2 | custom fusion | bytes 3244032 | tf_op jit(solution)/shard_map/gather | solution.py:102
  758.4 134.1 %gather_fusion.1 = bf16[12288,64]{1,0:T(8,128)(2,1)} fusion(bf16[4,12,256,64]{3,2,1,0:T(8,128)(2,1)S(1)} %reshape.1041, s32[12288]{0:T(1024)S(1)} %bitcast.199), kind=kCustom, calls=%fused_computation.1 | custom fusion | bytes 3293184 | tf_op jit(solution)/shard_map/gather | solution.py:101
  901.4 38.7 %fusion.2 = (bf16[1024,3072]{1,0:T(8,128)(2,1)}, f32[1024,3072]{1,0:T(8,128)}) fusion(f32[3072]{0:T(1024)S(1)} %convert_element_type.101, bf16[768,3072]{1,0:T(8,128)(2,1)} %all-gather.9.cloned.1.call-done, f32[1024,768]{0,1:T(8,128)S(1)} %get-tuple-element.249, f32[768]{0:T(1024)S(1)} %convert_element_type.99, f32[768]{0:T(1024)S(1)} %convert_element_type.98, ...), kind=kOutput, calls=%fused_computation.17 | convolution fusion | flops 5043388416 | bytes 26765312 | tf_op jit(solution)/shard_map/dot_general | solution.py:217
  954.7 12.9 convert_reduce_fusion
  981.0 32.5 %scatter_custom_fusion.5 = bf16[12288,64]{1,0:T(8,128)(2,1)S(1)} fusion(s32[12288]{0:T(1024)} %copy-done.27, bf16[12288,64]{1,0:T(8,128)(2,1)} %bitcast.228, bf16[]{:T(256)} %constant.338.clone.1), kind=kCustom, calls=%fused_computation.111 | custom fusion | bytes 1573376
  1042.7 32.5 %scatter_custom_fusion.4 = bf16[12288,64]{1,0:T(8,128)(2,1)S(1)} fusion(s32[12288]{0:T(1024)} %copy-done.28, bf16[12288,64]{1,0:T(8,128)(2,1)} %bitcast.229, bf16[]{:T(256)} %constant.338.clone.1), kind=kCustom, calls=%fused_computation.113 | custom fusion | bytes 1573376
  1088.8 33.3 %scatter_fusion.1 = bf16[12288,64]{1,0:T(8,128)(2,1)S(1)} fusion(bf16[12288,64]{1,0:T(8,128)(2,1)S(1)} %scatter_custom_fusion.4, s32[12288]{0:T(1024)S(1)} %copy-done.24, bf16[12288,64]{1,0:T(8,128)(2,1)} %reshape.1009), kind=kCustom, calls=%fused_computation.12 | custom fusion | bytes 4767744
  1174.1 300.1 %gather_fusion.3 = bf16[12288,192]{1,0:T(8,128)(2,1)} fusion(bf16[12,1024,192]{2,1,0:T(8,128)(2,1)} %pad_maximum_fusion, s32[12288]{0:T(1024)S(1)} %bitcast.204), kind=kCustom, calls=%fused_computation.3 | custom fusion | bytes 9535488 | tf_op jit(solution)/shard_map/gather | solution.py:91
  1490.4 10.5 fusion.91
  1511.4 25.4 %collective-permute-done.8 = bf16[2,1,12,49152]{3,0,2,1:T(2,128)(2,1)} collective-permute-done((bf16[2,1,12,49152]{3,0,2,1:T(2,128)(2,1)S(1)}, bf16[2,1,12,49152]{3,0,2,1:T(2,128)(2,1)}, u32[]{:S(2)}, u32[]{:S(2)}) %collective-permute-start.8) | collective-permute-done | bytes 2359328 | tf_op jit(solution)/shard_map/ppermute | solution.py:22
  1556.5 205.0 %gather_fusion.5 = bf16[12288,192]{1,0:T(8,128)(2,1)} fusion(bf16[12,1024,192]{2,1,0:T(8,128)(2,1)} %pad_maximum_fusion, s32[12288]{0:T(1024)S(1)} %bitcast.202), kind=kCustom, calls=%fused_computation.5 | custom fusion | bytes 9535488 | tf_op jit(solution)/shard_map/gather | solution.py:102
  1791.2 222.3 %gather_fusion.4 = bf16[12288,192]{1,0:T(8,128)(2,1)} fusion(bf16[4,12,256,192]{3,2,1,0:T(8,128)(2,1)} %reshape.1042, s32[12288]{0:T(1024)S(1)} %bitcast.200), kind=kCustom, calls=%fused_computation.4 | custom fusion | bytes 9584640 | tf_op jit(solution)/shard_map/gather | solution.py:101
  2065.0 41.5 %all-reduce.18 = (f32[768]{0:T(1024)S(1)}, f32[768]{0:T(1024)S(1)}, f32[768]{0:T(1024)S(1)}, f32[768]{0:T(1024)S(1)}, f32[768]{0:T(1024)S(1)}, /*index=5*/f32[30...) all-reduce(f32[768]{0:T(1024)S(1)} %slice.373, ...), channel_id=3, replica_groups=mesh['tok'=8,'grp'=4] {'tok','grp'}, use_global_device_ids=true, to_apply=%region_23.24.clone | all-reduce | flops 9216 | bytes 73728
  2123.0 59.9 %reduce-scatter.13.cloned.1.call-done = f32[24,2304]{1,0:T(8,128)} async-done(((f32[768,2304]{1,0:T(8,128)}), f32[24,2304]{1,0:T(8,128)}) %reduce-scatter.13.cloned.1.call-update) | async-done | bytes 221200
  (322 shorter events, 427.2 us)
Async XLA Ops:
  7.2 71.5 %all-gather.5.cloned.1.call-start = ((), (), s32[]{:S(2)}) async-start(), calls=%async_computation.4 | async-start | bytes 3649536 | tf_op jit(solution)/shard_map/all_gather | solution.py:139
  7.9 889.2 %all-gather.7.cloned.1.call-start = ((), (), s32[]{:S(2)}) async-start(), calls=%async_computation.5 | async-start | bytes 1216512 | tf_op jit(solution)/shard_map/all_gather | solution.py:142
  24.0 871.7 %copy-start.25 = (pred[12,1024]{1,0:T(8,128)(4,1)}, pred[12,1024]{1,0:T(8,128)(4,1)S(1)}, u32[]{:S(2)}) copy-start(pred[12,1024]{1,0:T(8,128)(4,1)S(1)} %get-tuple-element.228) | copy-start | bytes 36868
  25.8 732.6 %copy-start = (s32[12,1024,1]{1,2,0:T(1,128)}, s32[12,1024,1]{1,2,0:T(1,128)S(1)}, u32[]{:S(2)}) copy-start(s32[12,1024,1]{1,2,0:T(1,128)S(1)} %get-tuple-element.230) | copy-start | bytes 147460
  26.1 600.3 %copy-start.2 = (s32[12,1024,1]{1,2,0:T(1,128)}, s32[12,1024,1]{1,2,0:T(1,128)S(1)}, u32[]{:S(2)}) copy-start(s32[12,1024,1]{1,2,0:T(1,128)S(1)} %get-tuple-element.241) | copy-start | bytes 147460
  28.1 106.2 %copy-start.27 = (s32[12288]{0:T(1024)}, s32[12288]{0:T(1024)S(1)}, u32[]{:S(2)}) copy-start(s32[12288]{0:T(1024)S(1)} %reshape.983) | copy-start | bytes 147460
  205.4 55.3 %collective-permute-start.2 = (bf16[2,1,12,49152]{3,0,2,1:T(2,128)(2,1)S(1)}, bf16[2,1,12,49152]{3,0,2,1:T(2,128)(2,1)}, u32[]{:S(2)}, u32[]{:S(2)}) collective-permute-start(bf16[2,1,12,49152]{3,0,2,1:T(2,128)(2,1)S(1)} %copy.161), channel_id=1, source_target_pairs={{0,4},{4,0},{8,12},{12,8},{16,20},{20,16},{24,28},{28,24},{1,5},{5... | collective-permute-start | bytes 7077896 | tf_op jit(solution)/shard_map/ppermute | solution.py:22
  207.8 693.6 %all-gather.9.cloned.1.call-start = ((), (), s32[]{:S(2)}) async-start(), calls=%async_computation.6 | async-start | bytes 4866048 | tf_op jit(solution)/shard_map/all_gather | solution.py:146
  271.3 112.2 %collective-permute-start.3 = (bf16[1,2,12,49152]{3,1,2,0:T(2,128)(2,1)}, bf16[1,2,12,49152]{3,1,2,0:T(2,128)(2,1)S(1)}, u32[]{:S(2)}, u32[]{:S(2)}) collective-permute-start(bf16[1,2,12,49152]{3,1,2,0:T(2,128)(2,1)} %copy.163), channel_id=1, source_target_pairs={{0,8},{8,0},{4,12},{12,4},{16,24},{24,16},{20,28},{28,20},{1,9},{9... | collective-permute-start | bytes 7077896 | tf_op jit(solution)/shard_map/ppermute | solution.py:22
  318.5 3.9 collective-permute-start
  320.4 619.7 %all-gather.11.cloned.1.call-start = ((), (), s32[]{:S(2)}) async-start(), calls=%async_computation.7 | async-start | bytes 4866048 | tf_op jit(solution)/shard_map/all_gather | solution.py:148
  322.5 3.9 collective-permute-start.1
  326.6 143.5 %copy-start.4 = (s32[4,12,256,1]{2,3,1,0:T(1,128)}, s32[4,12,256,1]{2,3,1,0:T(1,128)S(1)}, u32[]{:S(2)}) copy-start(s32[4,12,256,1]{2,3,1,0:T(1,128)S(1)} %get-tuple-element.239) | copy-start | bytes 147460
  599.1 16.1 collective-permute-start.4
  620.8 130.4 %collective-permute-start.5 = (bf16[1,2,12,16384]{3,1,2,0:T(2,128)(2,1)}, bf16[1,2,12,16384]{3,1,2,0:T(2,128)(2,1)}, u32[]{:S(2)}, u32[]{:S(2)}) collective-permute-start(bf16[1,2,12,16384]{3,1,2,0:T(2,128)(2,1)} %copy.174), channel_id=1, source_target_pairs={{0,8},{8,0},{4,12},{12,4},{16,24},{24,16},{20,28},{28,20},{1,9},{9... | collective-permute-start | bytes 2359304 | tf_op jit(solution)/shard_map/ppermute | solution.py:22
  621.1 1501.9 %reduce-scatter.7.cloned.1.call-start = ((), (), s32[]{:S(2)}) async-start(), calls=%async_computation.8 | async-start | bytes 2433024 | tf_op jit(solution)/shard_map/reduce_scatter | solution.py:310
  900.9 73.9 %copy-start.10 = (f32[1024,768]{0,1:T(8,128)}, f32[1024,768]{0,1:T(8,128)S(1)}, u32[]{:S(2)}) copy-start(f32[1024,768]{0,1:T(8,128)S(1)} %get-tuple-element.249) | copy-start | bytes 9437188
  1020.4 14.9 collective-permute-start.6
  1041.0 39.5 %collective-permute-start.7 = (bf16[1,2,12,16384]{3,1,2,0:T(2,128)(2,1)}, bf16[1,2,12,16384]{3,1,2,0:T(2,128)(2,1)}, u32[]{:S(2)}, u32[]{:S(2)}) collective-permute-start(bf16[1,2,12,16384]{3,1,2,0:T(2,128)(2,1)} %copy.189), channel_id=1, source_target_pairs={{0,8},{8,0},{4,12},{12,4},{16,24},{24,16},{20,28},{28,20},{1,9},{9... | collective-permute-start | bytes 2359304 | tf_op jit(solution)/shard_map/ppermute | solution.py:22
  1080.4 1042.7 %reduce-scatter.9.cloned.1.call-start = ((), (), s32[]{:S(2)}) async-start(), calls=%async_computation.9 | async-start | bytes 9732096 | tf_op jit(solution)/shard_map/reduce_scatter | solution.py:314
  1489.1 47.7 %collective-permute-start.8 = (bf16[2,1,12,49152]{3,0,2,1:T(2,128)(2,1)S(1)}, bf16[2,1,12,49152]{3,0,2,1:T(2,128)(2,1)}, u32[]{:S(2)}, u32[]{:S(2)}) collective-permute-start(bf16[2,1,12,49152]{3,0,2,1:T(2,128)(2,1)S(1)} %copy.203), channel_id=1, source_target_pairs={{0,4},{4,0},{8,12},{12,8},{16,20},{20,16},{24,28},{28,24},{1,5},{5... | collective-permute-start | bytes 7077896 | tf_op jit(solution)/shard_map/ppermute | solution.py:22
  1500.9 622.1 %reduce-scatter.11.cloned.1.call-start = ((), (), s32[]{:S(2)}) async-start(), calls=%async_computation.10 | async-start | bytes 9732096 | tf_op jit(solution)/shard_map/reduce_scatter | solution.py:316
  1547.8 230.2 %collective-permute-start.9 = (bf16[1,2,12,49152]{3,1,2,0:T(2,128)(2,1)}, bf16[1,2,12,49152]{3,1,2,0:T(2,128)(2,1)S(1)}, u32[]{:S(2)}, u32[]{:S(2)}) collective-permute-start(bf16[1,2,12,49152]{3,1,2,0:T(2,128)(2,1)} %copy.205), channel_id=1, source_target_pairs={{0,8},{8,0},{4,12},{12,4},{16,24},{24,16},{20,28},{28,20},{1,9},{9... | collective-permute-start | bytes 7077896 | tf_op jit(solution)/shard_map/ppermute | solution.py:22
  1555.7 627.2 %reduce-scatter.13.cloned.1.call-start = ((), (), s32[]{:S(2)}) async-start(), calls=%async_computation.11 | async-start | bytes 7299072
  (45 other events, 604.8 us)
Sparse Core Ops, SparseCore 0:
  10.9 62.9 all-gather.4
  207.9 54.1 all-gather.6
  320.5 62.1 all-gather.8
  621.2 63.9 all-gather.10
  1080.5 98.7 reduce-scatter.6
  1501.0 159.8 reduce-scatter.8
  1667.4 135.0 reduce-scatter.10
  2061.4 121.4 reduce-scatter.12
where the time goes:
time: 2210 us; the launch traced here: 2190 us
  local copies, waits for them, and re-layouts  1720 us (78%)
  waiting for transfers between devices  152 us (7%)
  matrix products  150 us (7%)
  blocking collectives  84.4 us (4%)
  other arithmetic  55.7 us (3%)
    gather x2, local copies, waits for them, and re-layouts, collect(): taken = values[lanes, jnp.minimum(arrived_at, count - 1)]  421 us
    gather x5, local copies, waits for them, and re-layouts, restore(): shaped[jnp.minimum(send_slot, span - 1), lanes, jnp.clip(rank, 0, share -...  376 us
    unnamed x147, local copies, waits for them, and re-layouts  354 us
    gather x5, local copies, waits for them, and re-layouts, restore(): near_rows = values[lanes, own_at]  346 us
    ppermute x10, waiting for transfers between devices, swapped(): return lax.ppermute(block, axis, route)  90.8 us
    unnamed x2, blocking collectives  84.4 us
    unnamed x9, waiting for transfers between devices  60.7 us
    another operation x10, local copies, waits for them, and re-layouts, sectioned(): piece.reshape((span >> level + 1, 2, 1 << level) + piece.shape[1:])  59.6 us
  transfers between devices with their start and end apart: 18, of which 7 were waited for; matrix products, arithmetic and copies ran while one was open for 78% of the time, Pallas kernels for 0%

commit v1 on v0

v1 whole, which is shorter than its diff:
```python
import jax
import jax.numpy as jnp
from jax import lax
from jax.experimental import pallas as pl
from jax.experimental.pallas import tpu as pltpu
from jax.sharding import PartitionSpec as P

CL = 128
LONG = 4096
F32 = jnp.float32
BF = jnp.bfloat16
VMEM_ALL = 64 * 1024 * 1024 - 65536

epsilon = 1e-05
root_half = 0.7071067811865476
density_norm = 0.3989422804014327

def normalize(hidden, gain, shift):
    centred = hidden - jnp.mean(hidden, axis=1, keepdims=True)
    inverse_std = lax.rsqrt(jnp.mean(centred * centred, axis=1, keepdims=True) + epsilon)
    unit = centred * inverse_std
    return (unit * gain + shift, unit, inverse_std)


def normalize_back(grad_out, gain, unit, inverse_std):
    scaled = grad_out * gain
    return inverse_std * (
        scaled
        - jnp.mean(scaled, axis=1, keepdims=True)
        - unit * jnp.mean(scaled * unit, axis=1, keepdims=True)
    )


def nt(a,b): return lax.dot_general(a,b,(((1,),(1,)),((),())),preferred_element_type=F32)
def nn(a,b): return lax.dot_general(a,b,(((1,),(0,)),((),())),preferred_element_type=F32)
def tn(a,b): return lax.dot_general(a,b,(((0,),(0,)),((),())),preferred_element_type=F32)

def fwd_kernel(pos, tok, w, bias, att, left, right, src, ord_, oc):
    h=pl.program_id(0)
    n=tok.shape[0]
    ch=512
    def proj(i,_):
        r=pl.multiple_of(i*ch,ch)
        acc=nn(tok[pl.ds(r,ch),:],w[...])+bias[0]
        src[pl.ds(2*r,ch,stride=2),:]=acc[:,:128]
        src[pl.ds(2*r+1,ch,stride=2),:]=acc[:,128:]
        return 0
    lax.fori_loop(0,n//ch,proj,0)
    U=64
    def scat(i,_):
        for u in range(U):
            t=i*U+u
            ord_[pl.ds(2*pos[h*n+t],2),:]=src[pl.ds(2*t,2),:]
        return 0
    lax.fori_loop(0,n//U,scat,0)
    CB=4
    def clus(i,_):
        for u in range(CB):
            r=pl.multiple_of((i*CB+u)*CL,CL)
            l=ord_[pl.ds(2*r,CL,stride=2),:].astype(BF)
            rr=ord_[pl.ds(2*r+1,CL,stride=2),:].astype(BF)
            left[0,pl.ds(r,CL),:]=l
            right[0,pl.ds(r,CL),:]=rr
            s=nt(rr,l)
            m=jnp.max(s,axis=0,keepdims=True)
            e=jnp.exp((s-m)*0.125)
            p=(e*(1.0/jnp.sum(e,axis=0,keepdims=True))).astype(BF)
            oc[pl.ds(r,CL),:]=tn(p,rr)
        return 0
    lax.fori_loop(0,n//CL//CB,clus,0)
    def gath(i,_):
        for u in range(U):
            t=i*U+u
            src[pl.ds(t,1),:]=oc[pl.ds(pos[h*n+t],1),:]
        return 0
    lax.fori_loop(0,n//U,gath,0)
    att[0]=src[pl.ds(0,n),:].astype(BF)

def fwd(pos,tok,w,bias):
    n=tok.shape[0]; H=pos.shape[0]//n
    return pl.pallas_call(fwd_kernel,grid=(H,),
      out_shape=(jax.ShapeDtypeStruct((H,n,128),BF),)*3,
      in_specs=[pl.BlockSpec(memory_space=pltpu.SMEM),
                pl.BlockSpec((n,tok.shape[1]),lambda h:(0,0)),
                pl.BlockSpec((tok.shape[1],256),lambda h:(0,h)),
                pl.BlockSpec((1,1,256),lambda h: (h, 0, 0))],
      out_specs=(pl.BlockSpec((1,n,128),lambda h: (h, 0, 0)),)*3,
      scratch_shapes=[pltpu.VMEM((2*n,128),F32),pltpu.VMEM((2*n,128),F32),pltpu.VMEM((n,128),F32)],
      compiler_params=pltpu.CompilerParams(vmem_limit_bytes=VMEM_ALL),name="att_fwd")(pos,tok,w,bias)

def bwd_kernel(pos, left, right, g, gj, src, ord_, dc):
    h=pl.program_id(0)
    n=g.shape[1]
    U=64
    src[pl.ds(0,n),:]=g[0].astype(F32)
    def scat(i,_):
        for u in range(U):
            t=i*U+u
            ord_[pl.ds(pos[h*n+t],1),:]=src[pl.ds(t,1),:]
        return 0
    lax.fori_loop(0,n//U,scat,0)
    lane=lax.broadcasted_iota(jnp.int32,(CL,128),1)
    mask=(lane<64)==(h==0)
    CB=4
    def clus(i,_):
        for u in range(CB):
            r=pl.multiple_of((i*CB+u)*CL,CL)
            l=left[0,pl.ds(r,CL),:]
            rr=right[0,pl.ds(r,CL),:]
            d=jnp.where(mask,ord_[pl.ds(r,CL),:],0.0).astype(BF)
            s=nt(rr,l)
            m=jnp.max(s,axis=0,keepdims=True)
            e=jnp.exp((s-m)*0.125)
            p=e*(1.0/jnp.sum(e,axis=0,keepdims=True))
            dp=nt(rr,d)
            rd=jnp.sum(dp*p,axis=0,keepdims=True)
            ds=(p*(dp-rd)).astype(BF)
            dl=tn(ds,rr)*0.125
            dr=nn(ds,l)*0.125+nn(p.astype(BF),d)
            dc[pl.ds(2*r,CL,stride=2),:]=dl
            dc[pl.ds(2*r+1,CL,stride=2),:]=dr
        return 0
    lax.fori_loop(0,n//CL//CB,clus,0)
    def gath(i,_):
        for u in range(U):
            t=i*U+u
            src[pl.ds(2*t,2),:]=dc[pl.ds(2*pos[h*n+t],2),:]
        return 0
    lax.fori_loop(0,n//U,gath,0)
    ch=512
    def out(i,_):
        r=pl.multiple_of(i*ch,ch)
        gj[0,pl.ds(r,ch),:128]=src[pl.ds(2*r,ch,stride=2),:].astype(BF)
        gj[0,pl.ds(r,ch),128:]=src[pl.ds(2*r+1,ch,stride=2),:].astype(BF)
        return 0
    lax.fori_loop(0,n//ch,out,0)

def bwd(pos,left,right,g):
    n=g.shape[1]; H=left.shape[0]
    blk=lambda: pl.BlockSpec((1,n,128),lambda h: (h, 0, 0))
    return pl.pallas_call(bwd_kernel,grid=(H,),
      out_shape=jax.ShapeDtypeStruct((H,n,256),BF),
      in_specs=[pl.BlockSpec(memory_space=pltpu.SMEM),blk(),blk(),pl.BlockSpec((1,n,128),lambda h: (h // 2, 0, 0))],
      out_specs=pl.BlockSpec((1,n,256),lambda h: (h, 0, 0)),
      scratch_shapes=[pltpu.VMEM((2*n,128),F32),pltpu.VMEM((n,128),F32),pltpu.VMEM((2*n,128),F32)],
      compiler_params=pltpu.CompilerParams(vmem_limit_bytes=VMEM_ALL),name="att_bwd")(pos,left,right,g)

def flip(block, mask):
    count = lax.axis_size("tok")
    return lax.ppermute(block, "tok", [(i, i ^ mask) for i in range(count)])


def gather_all(item):
    return lax.all_gather(item, ("tok", "grp"), axis=0, tiled=True)


def scatter_sum(item):
    return lax.psum_scatter(item, ("tok", "grp"), scatter_dimension=0, tiled=True)


def shards(
    tokens,
    upstream,
    cluster_pos,
    project_in,
    query_bias,
    value_bias,
    project_out,
    output_bias,
    first_gain,
    first_shift,
    expand,
    expand_bias,
    contract,
    contract_bias,
    second_gain,
    second_shift,
):
    inputs = tokens[0]
    count, width = inputs.shape
    positions = cluster_pos[0] % LONG
    heads = positions.shape[0]
    head_dim = width // heads
    span = LONG // count
    mine = heads // span
    offset = lax.axis_index("tok") % span
    total = span * count

    near = flip(inputs, 1)
    far = flip(jnp.stack([inputs, near]), 2)
    block = jnp.concatenate([inputs[None], near[None], far]).reshape(total, width)
    near_at = flip(positions, 1)
    far_at = flip(jnp.stack([positions, near_at]), 2)
    block_at = jnp.concatenate([positions[None], near_at[None], far_at])
    own_at = lax.dynamic_slice_in_dim(block_at, offset * mine, mine, axis=1)
    own_at = own_at.transpose(1, 0, 2).reshape(-1)

    project_in = gather_all(project_in)
    project_out = gather_all(project_out)
    expand = gather_all(expand)
    contract = gather_all(contract)
    packed = jnp.concatenate(
        [
            query_bias, value_bias, output_bias, first_gain, first_shift,
            contract_bias, second_gain, second_shift, expand_bias,
        ]
    )
    few = query_bias.shape[0]
    packed = gather_all(packed[None].astype(F32))
    vectors = [packed[:, i * few : (i + 1) * few].reshape(-1) for i in range(8)]
    query_bias, value_bias, output_bias, gain_one, shift_one, contract_bias, gain_two, shift_two = vectors
    expand_bias = packed[:, 8 * few :].reshape(-1)

    pieces = lax.dynamic_slice_in_dim(
        project_in.reshape(width, 3, heads, head_dim), offset * mine, mine, axis=2
    )
    hollow = jnp.zeros((width, head_dim), BF)
    columns = []
    for h in range(mine):
        query, key, value = pieces[:, 0, h], pieces[:, 1, h], pieces[:, 2, h]
        columns += [hollow, query, value, key] if h == 0 else [query, hollow, key, value]
    arranged = jnp.concatenate(columns, axis=1)
    own_query = lax.dynamic_slice_in_dim(query_bias.reshape(heads, head_dim), offset * mine, mine)
    own_value = lax.dynamic_slice_in_dim(value_bias.reshape(heads, head_dim), offset * mine, mine)
    blank = jnp.zeros((head_dim,), F32)
    rows = []
    for h in range(mine):
        parts = [blank, own_query[h], own_value[h], blank] if h == 0 else [own_query[h], blank, blank, own_value[h]]
        rows.append(jnp.concatenate(parts))
    bias_rows = jnp.stack(rows)[:, None]

    att, left, right = fwd(own_at, block, arranged, bias_rows)
    lane = jnp.arange(2 * head_dim) < head_dim
    pair = jnp.where(lane, att[0], att[1]).reshape(span, count, 2 * head_dim)
    single = att[2, :, head_dim:].reshape(span, 2, count // 2, head_dim)
    single = single.transpose(0, 2, 1, 3).reshape(span, count // 2, 2 * head_dim)
    leaving = jnp.concatenate([pair, single], axis=1)
    came = [leaving[0]] + [flip(leaving[k], k) for k in range(1, span)]

    def open_single(item):
        return jnp.concatenate([item[:, :head_dim], item[:, head_dim:]], axis=0)

    merged = jnp.concatenate(
        [item[:count] for item in came] + [open_single(item[count:]) for item in came], axis=1
    )
    by_owner = project_out.reshape(span, mine * head_dim, width)
    turned = [lax.dynamic_index_in_dim(by_owner, offset ^ k, 0, False) for k in range(span)]
    project_turned = jnp.concatenate(
        [item[: 2 * head_dim] for item in turned] + [item[2 * head_dim :] for item in turned], axis=0
    )

    branch = jnp.dot(merged, project_turned, preferred_element_type=F32) + output_bias
    normed_one, unit_one, inverse_one = normalize(inputs.astype(F32) + branch, gain_one, shift_one)
    normed_low = normed_one.astype(BF)
    inner = jnp.dot(normed_low, expand, preferred_element_type=F32) + expand_bias
    lifted = jax.nn.gelu(inner, approximate=False).astype(BF)
    second_sum = normed_one + jnp.dot(lifted, contract, preferred_element_type=F32) + contract_bias
    result, unit_two, inverse_two = normalize(second_sum, gain_two, shift_two)
    cotangent = upstream[0].astype(F32)
    second_gain_grad = jnp.sum(cotangent * unit_two, axis=0)
    second_shift_grad = jnp.sum(cotangent, axis=0)
    grad_second = normalize_back(cotangent, gain_two, unit_two, inverse_two)
    grad_mid = grad_second.astype(BF)
    contract_bias_grad = jnp.sum(grad_mid.astype(F32), axis=0)
    contract_grad = jnp.einsum("rf,rd->fd", lifted, grad_mid, preferred_element_type=F32)
    grad_lifted = jnp.einsum("rd,fd->rf", grad_mid, contract, preferred_element_type=F32)
    slope = (
        0.5 * (1.0 + lax.erf(inner * root_half))
        + inner * jnp.exp(-0.5 * inner * inner) * density_norm
    )
    grad_inner = (grad_lifted * slope).astype(BF)
    expand_bias_grad = jnp.sum(grad_inner.astype(F32), axis=0)
    expand_grad = jnp.einsum("rd,rf->df", normed_low, grad_inner, preferred_element_type=F32)
    grad_normed = grad_second + jnp.einsum(
        "rf,df->rd", grad_inner, expand, preferred_element_type=F32
    )
    first_gain_grad = jnp.sum(grad_normed * unit_one, axis=0)
    first_shift_grad = jnp.sum(grad_normed, axis=0)
    grad_first = normalize_back(grad_normed, gain_one, unit_one, inverse_one)
    grad_branch = grad_first.astype(BF)
    output_bias_grad = jnp.sum(grad_branch.astype(F32), axis=0)
    turned_grad = jnp.einsum("rd,re->de", merged, grad_branch, preferred_element_type=F32)
    grad_merged = jnp.einsum(
        "re,de->rd", grad_branch, project_turned, preferred_element_type=F32
    ).astype(BF)

    pair_cols = span * 2 * head_dim
    sending = []
    for k in range(span):
        two = grad_merged[:, k * 2 * head_dim : (k + 1) * 2 * head_dim]
        one = grad_merged[:, pair_cols + k * head_dim : pair_cols + (k + 1) * head_dim]
        one = jnp.concatenate([one[: count // 2], one[count // 2 :]], axis=1)
        sending.append(jnp.concatenate([two, one], axis=0))
    landed = [sending[0]] + [flip(sending[k], k) for k in range(1, span)]
    grad_pair = jnp.concatenate([item[:count] for item in landed], axis=0)
    grad_single = jnp.concatenate([open_single(item[count:]) for item in landed], axis=0)
    grad_att = jnp.stack([grad_pair, jnp.concatenate([grad_single, grad_single], axis=1)])
    grad_rows = bwd(own_at, left, right, grad_att)

    arranged_grad = jnp.concatenate(
        [jnp.einsum("rd,re->de", block, grad_rows[h], preferred_element_type=F32) for h in range(mine)],
        axis=1,
    ).reshape(width, mine, 4, head_dim)
    sums = jnp.sum(grad_rows.astype(F32), axis=1).reshape(mine, 4, head_dim)
    query_at = [1] + [0] * (mine - 1)
    key_at = [3] + [2] * (mine - 1)
    value_at = [2] + [3] * (mine - 1)

    def spread(take, at):
        return jnp.stack([take(h, at[h]) for h in range(mine)], axis=-2)

    own_grad = jnp.stack(
        [spread(lambda h, s: arranged_grad[:, h, s], at) for at in (query_at, key_at, value_at)], axis=1
    )
    project_in_grad = lax.dynamic_update_slice_in_dim(
        jnp.zeros((width, 3, heads, head_dim), F32), own_grad, offset * mine, axis=2
    ).reshape(width, 3 * width)
    own_sums = jnp.stack([spread(lambda h, s: sums[h, s], at) for at in (query_at, value_at)])
    bias_grads = lax.dynamic_update_slice_in_dim(
        jnp.zeros((2, heads, head_dim), F32), own_sums, offset * mine, axis=1
    ).reshape(2, width)
    partial = sum(
        jnp.einsum(
            "re,de->rd", grad_rows[h], arranged[:, 256 * h : 256 * h + 256], preferred_element_type=F32
        )
        for h in range(mine)
    ).reshape(span, count, width)
    token_grad = grad_first + partial[0]
    for k in range(1, span):
        token_grad = token_grad + flip(partial[k].astype(BF), k).astype(F32)

    by_owner = jnp.concatenate(
        [
            turned_grad[:pair_cols].reshape(span, 2 * head_dim, width),
            turned_grad[pair_cols:].reshape(span, head_dim, width),
        ],
        axis=1,
    )
    project_out_grad = jnp.concatenate(
        [lax.dynamic_index_in_dim(by_owner, offset ^ k, 0, False) for k in range(span)], axis=0
    )
    project_in_grad = scatter_sum(project_in_grad.astype(BF)).astype(F32)
    project_out_grad = scatter_sum(project_out_grad.astype(BF)).astype(F32)
    expand_grad = scatter_sum(expand_grad.astype(BF)).astype(F32)
    contract_grad = scatter_sum(contract_grad.astype(BF)).astype(F32)
    devices = lax.axis_size("tok") * lax.axis_size("grp")
    small = jnp.concatenate(
        [
            item.reshape(devices, -1)
            for item in (
                bias_grads[0], bias_grads[1], output_bias_grad, first_gain_grad, first_shift_grad,
                contract_bias_grad, second_gain_grad, second_shift_grad, expand_bias_grad,
            )
        ],
        axis=1,
    )
    small = scatter_sum(small)[0]
    each = [small[i * few : (i + 1) * few] for i in range(8)] + [small[8 * few :]]
    return (
        result.astype(BF)[None],
        token_grad[None],
        project_in_grad,
        each[0],
        each[1],
        project_out_grad,
        each[2],
        each[3],
        each[4],
        expand_grad,
        each[8],
        contract_grad,
        each[5],
        each[6],
        each[7],
    )


def solution(mesh):
    placed = (
        P("grp", "tok", None),
        P("grp", "tok", None),
        P("grp", None, "tok"),
        P(("tok", "grp"), None),
        P(("tok", "grp")),
        P(("tok", "grp")),
        P(("tok", "grp"), None),
        P(("tok", "grp")),
        P(("tok", "grp")),
        P(("tok", "grp")),
        P(("tok", "grp"), None),
        P(("tok", "grp")),
        P(("tok", "grp"), None),
        P(("tok", "grp")),
        P(("tok", "grp")),
        P(("tok", "grp")),
    )
    return jax.shard_map(
        shards,
        mesh=mesh,
        in_specs=placed,
        out_specs=(
            P("grp", "tok", None),
            P("grp", "tok", None),
            P(("tok", "grp"), None),
            P(("tok", "grp")),
            P(("tok", "grp")),
            P(("tok", "grp"), None),
            P(("tok", "grp")),
            P(("tok", "grp")),
            P(("tok", "grp")),
            P(("tok", "grp"), None),
            P(("tok", "grp")),
            P(("tok", "grp"), None),
            P(("tok", "grp")),
            P(("tok", "grp")),
            P(("tok", "grp")),
        ),
        check_vma=False,
    )
```

time: 2210 us -> 894 us (0.40)
  local copies, waits for them, and re-layouts: 1720 us -> 89.6 us
  Pallas kernels: 0 us -> 139 us
  blocking collectives: 84.4 us -> 208 us
  waiting for transfers between devices: 152 us -> 232 us
    gather x12 -> x0, local copies, waits for them, and re-layouts: 1140 us -> none  [the longest x2 421 us: collect(): taken = values[lanes, jnp.minimum(arrived_at, count - 1)]]
    unnamed x147 -> x169, local copies, waits for them, and re-layouts: 354 us -> 45.3 us
    reduce_scatter x3, waiting for transfers between devices: 0.01 us -> 156 us  [scatter_sum(): lax.psum_scatter(item, ('tok', 'grp'), scatter_dimension=0, tiled=True)]
    pallas_call x0 -> x2, Pallas kernels: none -> 139 us  [the longest x1 73.6 us: fwd(): pl.pallas_call(fwd_kernel, grid=(H,), out_shape=(jax.ShapeDtypeStruct((H,...]
    all_gather x0 -> x1, blocking collectives: none -> 120 us  [gather_all(): return lax.all_gather(item, ('tok', 'grp'), axis=0, tiled=True)]
    another operation x19 -> x8, local copies, waits for them, and re-layouts: 90.7 us -> 1.49 us  [the longest x1 1.13 us: shards(): single = att[2, :, head_dim:].reshape(span, 2, count // 2, head_dim)]
    unnamed x9, waiting for transfers between devices: 60.7 us -> 2.14 us
    reshape x4 -> x9, local copies, waits for them, and re-layouts: 44.6 us -> 1.95 us  [the longest x1 1.31 us: shards(): single.transpose(0, 2, 1, 3).reshape(span, count // 2, 2 * head_dim)]
  transfers between devices with their start and end apart: 18 -> 21, of which waited for: 7 -> 8; matrix products, arithmetic and copies ran while one was open for 78% -> 24% of each run, Pallas kernels for 0% -> 16%
where the time goes in v1:
time: 894 us; the launch traced here: 879 us
  waiting for transfers between devices  232 us (26%)
  blocking collectives  208 us (23%)
  matrix products  140 us (16%)
  Pallas kernels  139 us (16%)
  local copies, waits for them, and re-layouts  89.6 us (10%)
  other arithmetic  36.9 us (4%)
  starting transfers between devices  17.9 us (2%)
  between operations  15.8 us (2%)
    reduce_scatter x3, waiting for transfers between devices, scatter_sum(): lax.psum_scatter(item, ('tok', 'grp'), scatter_dimension=0, tiled=True)  156 us
    all_gather x1, blocking collectives, gather_all(): return lax.all_gather(item, ('tok', 'grp'), axis=0, tiled=True)  120 us
    unnamed x1, blocking collectives  88.7 us
    ppermute x13, waiting for transfers between devices, flip(): return lax.ppermute(block, 'tok', [(i, i ^ mask) for i in range(count)])  73.7 us
    pallas_call x1, Pallas kernels, fwd(): pl.pallas_call(fwd_kernel, grid=(H,), out_shape=(jax.ShapeDtypeStruct((H,...  73.6 us
    pallas_call x1, Pallas kernels, bwd(): pl.pallas_call(bwd_kernel, grid=(H,), out_shape=jax.ShapeDtypeStruct((H,...  65.1 us
    unnamed x169, local copies, waits for them, and re-layouts  45.3 us
    dot_general x1, matrix products, shards(): jnp.dot(normed_low, expand, preferred_element_type=F32) + expand_bias  39.6 us
  transfers between devices with their start and end apart: 21, of which 8 were waited for; matrix products, arithmetic and copies ran while one was open for 24% of the time, Pallas kernels for 16%

profile of v1, /device:TPU:0, one launch (start us, length us, event | category | flops | bytes accessed | tf_op | source)
XLA Modules:
  0.0 878.7 jit_solution(4533807791893603135)
XLA Ops:
  14.2 35.2 %collective-permute-done.2 = bf16[1024,768]{0,1:T(8,128)(2,1)S(1)} collective-permute-done((bf16[1024,768]{0,1:T(8,128)(2,1)S(1)}, bf16[1024,768]{0,1:T(8,128)(2,1)S(1)}, u32[]{:S(2)}, u32[]{:S(2)}) %collective-permute-start.2) | collective-permute-done | bytes 1572896 | tf_op jit(solution)/shard_map/ppermute | solution.py:150
  55.2 119.7 %all-gather = f32[32,1,288]{2,1,0:T(1,128)S(1)} all-gather(f32[1,1,288]{2,1,0:T(1,128)S(1)} %bitcast_convert_fusion), channel_id=1, replica_groups=mesh['tok'=8,'grp'=4] {'tok','grp'}, dimensions={0}, use_global_device_ids=true | all-gather | bytes 38016 | tf_op jit(solution)/shard_map/all_gather | solution.py:154
  184.1 10.1 %collective-permute-done.1 = s32[2,12,1024]{2,0,1:T(2,128)S(1)} collective-permute-done((s32[2,12,1024]{2,0,1:T(2,128)S(1)}, s32[2,12,1024]{2,0,1:T(2,128)S(1)}, u32[]{:S(2)}, u32[]{:S(2)}) %collective-permute-start.1) | collective-permute-done | bytes 98336 | tf_op jit(solution)/shard_map/ppermute | solution.py:150
  207.5 5.0 pad_maximum_fusion
  212.5 8.7 copy.67
  239.7 73.6 %att_fwd.1 = (bf16[3,4096,128]{2,1,0:T(8,128)(2,1)}, bf16[3,4096,128]{2,1,0:T(8,128)(2,1)}, bf16[3,4096,128]{2,1,0:T(8,128)(2,1)}) custom-call(s32[12288]{0:T(1024)} %bitcast.285, bf16[4096,768]{1,0:T(8,128)(2,1)} %bitcast.237, bf16[768,768]{1,0:T(8,128)(2,1)} %concatenate.119.w, f32[3,1,256]{2,1,0:T(1,128)} %broadcast_in_dim.46.bias), custom_call_target="tpu_custom_call" | custom-call | tf_op jit(solution)/shard_map/att_fwd/pallas_call | solution.py:81
  325.3 7.6 collective-permute-done.6
  350.9 39.6 %fusion.2 = (bf16[1024,3072]{1,0:T(8,128)(2,1)}, f32[1024,3072]{1,0:T(8,128)}) fusion(f32[3072]{0:T(1024)S(1)} %copy-done.44, bf16[768,3072]{1,0:T(8,128)(2,1)} %all-gather.10.cloned.1.call-done, f32[1024,768]{0,1:T(8,128)} %copy-done.6, f32[768]{0:T(1024)S(1)} %copy-done.45, f32[768]{0:T(1024)S(1)} %copy-done.35, f32[1024]{0:T(1024)S(1)} %add_rsqrt_fusion.1, ...), kind=kOutput, calls=%fused_computation.4 | convolution fusion | flops 5043388416 | bytes 26765312 | tf_op jit(solution)/shard_map/dot_general | solution.py:255
  390.6 8.9 %fusion.105 = (f32[1024]{0:T(1024)S(1)}, f32[1024,768]{0,1:T(8,128)S(1)}) fusion(f32[768]{0:T(1024)S(1)} %copy-done.49, bf16[1024,3072]{1,0:T(8,128)(2,1)} %get-tuple-element.160, bf16[3072,768]{1,0:T(8,128)(2,1)} %all-gather.12.cloned.1.call-done, f32[768]{0:T(1024)S(1)} %copy-done.45, f32[768]{0:T(1024)S(1)} %copy-done.35, ...), kind=kOutput, calls=%fused_computation.254 | convolution fusion | flops 4837342208 | bytes 17323008 | tf_op jit(solution)/shard_map/dot_general | solution.py:257
  406.1 13.0 %convert_reduce_fusion = (f32[3072]{0:T(1024)}, bf16[1024,3072]{1,0:T(8,128)(2,1)S(1)}) fusion(f32[1024,3072]{1,0:T(8,128)} %get-tuple-element.161, f32[3072]{0:T(1024)S(1)} %copy-done.44, bf16[1024,768]{0,1:T(8,128)(2,1)S(1)} %get-tuple-element.74, bf16[3072,768]{1,0:T(8,128)(2,1)S(1)} %copy-done.61), kind=kOutput, calls=%fused_computation.11 | convolution fusion | flops 4872729600 | bytes 25190400 | tf_op jit(solution)/shard_map/rd,fd->rf/dot_general | solution.py:266
  419.1 7.2 multiply_reduce_fusion
  438.4 15.8 %collective-permute-done.7 = bf16[1536,128]{1,0:T(8,128)(2,1)S(1)} collective-permute-done((bf16[1536,128]{1,0:T(8,128)(2,1)S(1)}, bf16[1536,128]{1,0:T(8,128)(2,1)S(1)}, u32[]{:S(2)}, u32[]{:S(2)}) %collective-permute-start.7) | collective-permute-done | bytes 393248 | tf_op jit(solution)/shard_map/ppermute | solution.py:150
  456.9 65.1 %att_bwd.1 = bf16[3,4096,256]{2,1,0:T(8,128)(2,1)} custom-call(s32[12288]{0:T(1024)} %bitcast.286, bf16[3,4096,128]{2,1,0:T(8,128)(2,1)} %get-tuple-element.19.left, bf16[3,4096,128]{2,1,0:T(8,128)(2,1)} %get-tuple-element.20.right, bf16[2,4096,128]{2,1,0:T(8,128)(2,1)} %pad_maximum_fusion.3.g), custom_call_target="tpu_custom_call" | custom-call | tf_op jit(solution)/shard_map/att_bwd/pallas_call | solution.py:141
  522.0 5.4 fusion.30
  540.9 9.9 %convolution_convert_fusion.1 = bf16[768,3072]{1,0:T(8,128)(2,1)} fusion(bf16[1024,3072]{1,0:T(8,128)(2,1)} %copy-done.62, f32[1024,768]{0,1:T(8,128)S(1)} %copy-done.8, f32[768]{0:T(1024)S(1)} %copy-done.46, f32[768]{0:T(1024)S(1)} %copy-done.36, f32[1024]{0:T(1024)S(1)} %copy-done.42, f32[1024]{0:T(1024)S(1)} %copy-done.34), kind=kOutput, calls=%fused_computation.31 | convolution fusion | flops 4838129664 | bytes 14170112 | tf_op jit(solution)/shard_map/rd,rf->df/dot_general | solution.py:273
  552.2 9.9 %convolution_convert_fusion = bf16[3072,768]{1,0:T(8,128)(2,1)} fusion(bf16[1024,3072]{1,0:T(8,128)(2,1)} %get-tuple-element.160, bf16[1024,768]{0,1:T(8,128)(2,1)S(1)} %copy-done.30), kind=kOutput, calls=%fused_computation.30 | convolution fusion | flops 4834197504 | bytes 12582912 | tf_op jit(solution)/shard_map/rf,rd->fd/dot_general | solution.py:265
  563.1 8.4 fusion.33
  571.6 6.5 fusion.31
  578.0 16.7 %fusion.106 = (bf16[4096,768]{0,1:T(8,128)(2,1)}, f32[4096,768]{0,1:T(8,128)}) fusion(bf16[768,64]{1,0:T(8,128)(2,1)S(1)} %copy-done.10, bf16[768,64]{1,0:T(8,128)(2,1)} %bitcast.260, bf16[768,64]{1,0:T(8,128)(2,1)} %bitcast.258, bf16[768,64]{1,0:T(8,128)(2,1)S(1)} %bitcast.256, bf16[3,4096,256]{2,1,0:T(8,128)(2,1)S(1)} %bitcast.236, ...), kind=kOutput, calls=%fused_computation.255 | convolution fusion | flops 1621622784 | bytes 46727168 | tf_op jit(solution)/shard_map/re,de->rd/dot_general | solution.py:323
  594.8 4.9 fusion.94
  609.9 88.7 %all-reduce = f32[32,288]{1,0:T(8,128)S(1)} all-reduce(f32[32,288]{1,0:T(8,128)S(1)} %concatenate.153), channel_id=3, replica_groups=mesh['tok'=8,'grp'=4] {'tok','grp'}, use_global_device_ids=true, to_apply=%region_17.18.clone | all-reduce | flops 9216 | bytes 73728
  702.4 5.5 fusion.28
  712.4 45.5 %reduce-scatter.9.cloned.1.call-done = bf16[24,3072]{1,0:T(8,128)(2,1)} async-done(((bf16[768,3072]{1,0:T(8,128)(2,1)}), bf16[24,3072]{1,0:T(8,128)(2,1)}) %reduce-scatter.9.cloned.1.call-update) | async-done | bytes 147472 | tf_op jit(solution)/shard_map/reduce_scatter | solution.py:158
  759.6 110.3 %reduce-scatter.11.cloned.1.call-done = bf16[96,768]{1,0:T(8,128)(2,1)} async-done(((bf16[3072,768]{1,0:T(8,128)(2,1)}), bf16[96,768]{1,0:T(8,128)(2,1)}) %reduce-scatter.11.cloned.1.call-update) | async-done | bytes 147472 | tf_op jit(solution)/shard_map/reduce_scatter | solution.py:158
  (337 shorter events, 141.9 us)
Async XLA Ops:
  7.2 187.7 %all-gather.8.cloned.1.call-start = ((), (), s32[]{:S(2)}) async-start(), calls=%async_computation.5 | async-start | bytes 1216512 | tf_op jit(solution)/shard_map/all_gather | solution.py:154
  7.9 213.2 %all-gather.6.cloned.1.call-start = ((), (), s32[]{:S(2)}) async-start(), calls=%async_computation.4 | async-start | bytes 3649536 | tf_op jit(solution)/shard_map/all_gather | solution.py:154
  8.7 342.2 %all-gather.10.cloned.1.call-start = ((), (), s32[]{:S(2)}) async-start(), calls=%async_computation.6 | async-start | bytes 4866048 | tf_op jit(solution)/shard_map/all_gather | solution.py:154
  9.4 381.2 %all-gather.12.cloned.1.call-start = ((), (), s32[]{:S(2)}) async-start(), calls=%async_computation.7 | async-start | bytes 4866048 | tf_op jit(solution)/shard_map/all_gather | solution.py:154
  11.2 196.3 %copy-start.3 = (bf16[1,1024,768]{1,2,0:T(8,128)(2,1)}, bf16[1,1024,768]{1,2,0:T(8,128)(2,1)S(1)}, u32[]{:S(2)}) copy-start(bf16[1,1024,768]{1,2,0:T(8,128)(2,1)S(1)} %copy.64) | copy-start | bytes 4718596
  11.2 38.2 %collective-permute-start.2 = (bf16[1024,768]{0,1:T(8,128)(2,1)S(1)}, bf16[1024,768]{0,1:T(8,128)(2,1)S(1)}, u32[]{:S(2)}, u32[]{:S(2)}) collective-permute-start(bf16[1024,768]{0,1:T(8,128)(2,1)S(1)} %bitcast.244), channel_id=1, source_target_pairs={{0,4},{4,0},{8,12},{12,8},{16,20},{20,16},{24,28},{28,24},{1,5},{5... | collective-permute-start | bytes 4718600 | tf_op jit(solution)/shard_map/ppermute | solution.py:150
  51.4 156.0 %collective-permute-start.3 = (bf16[2,1024,768]{1,2,0:T(8,128)(2,1)}, bf16[2,1024,768]{1,2,0:T(8,128)(2,1)}, u32[]{:S(2)}, u32[]{:S(2)}) collective-permute-start(bf16[2,1024,768]{1,2,0:T(8,128)(2,1)} %pad_maximum_fusion.1), channel_id=1, source_target_pairs={{0,8},{4,12},{8,0},{12,4},{16,24},{20,28},{24,16},{28,20},{1,9},{5... | collective-permute-start | bytes 9437192 | tf_op jit(solution)/shard_map/ppermute | solution.py:150
  53.3 130.1 %collective-permute-start = (s32[12,1024]{1,0:T(8,128)S(1)}, s32[12,1024]{1,0:T(8,128)S(1)}, u32[]{:S(2)}, u32[]{:S(2)}) collective-permute-start(s32[12,1024]{1,0:T(8,128)S(1)} %add_select_fusion), channel_id=1, source_target_pairs={{0,4},{4,0},{8,12},{12,8},{16,20},{20,16},{24,28},{28,24},{1,5},{5... | collective-permute-start | bytes 147464 | tf_op jit(solution)/shard_map/ppermute | solution.py:150
  54.9 644.9 %reduce-scatter.7.cloned.1.call-start = ((), (), s32[]{:S(2)}) async-start(), calls=%async_computation.8 | async-start | bytes 1216512 | tf_op jit(solution)/shard_map/reduce_scatter | solution.py:158
  183.5 10.7 %collective-permute-start.1 = (s32[2,12,1024]{2,0,1:T(2,128)S(1)}, s32[2,12,1024]{2,0,1:T(2,128)S(1)}, u32[]{:S(2)}, u32[]{:S(2)}) collective-permute-start(s32[2,12,1024]{2,0,1:T(2,128)S(1)} %pad_add_fusion), channel_id=1, source_target_pairs={{0,8},{4,12},{8,0},{12,4},{16,24},{20,28},{24,16},{28,20},{1,9},{5... | collective-permute-start | bytes 294920 | tf_op jit(solution)/shard_map/ppermute | solution.py:150
  320.0 12.9 %collective-permute-start.6 = (bf16[1536,128]{1,0:T(8,128)(2,1)S(1)}, bf16[1536,128]{1,0:T(8,128)(2,1)S(1)}, u32[]{:S(2)}, u32[]{:S(2)}) collective-permute-start(bf16[1536,128]{1,0:T(8,128)(2,1)S(1)} %get-tuple-element.102), channel_id=1, source_target_pairs={{0,12},{4,8},{8,4},{12,0},{16,28},{20,24},{24,20},{28,16},{1,13},{... | collective-permute-start | bytes 1179656 | tf_op jit(solution)/shard_map/ppermute | solution.py:150
  320.0 16.6 %collective-permute-start.5 = (bf16[1536,128]{1,0:T(8,128)(2,1)S(1)}, bf16[1536,128]{1,0:T(8,128)(2,1)S(1)}, u32[]{:S(2)}, u32[]{:S(2)}) collective-permute-start(bf16[1536,128]{1,0:T(8,128)(2,1)S(1)} %get-tuple-element.103), channel_id=1, source_target_pairs={{0,8},{4,12},{8,0},{12,4},{16,24},{20,28},{24,16},{28,20},{1,9},{5... | collective-permute-start | bytes 1179656 | tf_op jit(solution)/shard_map/ppermute | solution.py:150
  320.0 19.7 %collective-permute-start.4 = (bf16[1536,128]{1,0:T(8,128)(2,1)}, bf16[1536,128]{1,0:T(8,128)(2,1)S(1)}, u32[]{:S(2)}, u32[]{:S(2)}) collective-permute-start(bf16[1536,128]{1,0:T(8,128)(2,1)} %get-tuple-element.104), channel_id=1, source_target_pairs={{0,4},{4,0},{8,12},{12,8},{16,20},{20,16},{24,28},{28,24},{1,5},{5... | collective-permute-start | bytes 1179656 | tf_op jit(solution)/shard_map/ppermute | solution.py:150
  348.8 77.5 %copy-start.33 = (f32[1024]{0:T(1024)}, f32[1024]{0:T(1024)S(1)}, u32[]{:S(2)}) copy-start(f32[1024]{0:T(1024)S(1)} %broadcast_multiply_fusion.5) | copy-start | bytes 12292
  350.8 75.5 %copy-start.41 = (f32[1024]{0:T(1024)}, f32[1024]{0:T(1024)S(1)}, u32[]{:S(2)}) copy-start(f32[1024]{0:T(1024)S(1)} %add_rsqrt_fusion.1) | copy-start | bytes 12292
  434.1 276.1 %reduce-scatter.13.cloned.1.call-start = ((), (), s32[]{:S(2)}) async-start(), calls=%async_computation.11 | async-start | bytes 3649536
  434.5 20.0 %collective-permute-start.9 = (bf16[1536,128]{1,0:T(8,128)(2,1)S(1)}, bf16[1536,128]{1,0:T(8,128)(2,1)S(1)}, u32[]{:S(2)}, u32[]{:S(2)}) collective-permute-start(bf16[1536,128]{1,0:T(8,128)(2,1)S(1)} %maximum_maximum_fusion.2), channel_id=1, source_target_pairs={{0,12},{4,8},{8,4},{12,0},{16,28},{20,24},{24,20},{28,16},{1,13},{... | collective-permute-start | bytes 1179656 | tf_op jit(solution)/shard_map/ppermute | solution.py:150
  435.1 19.1 %collective-permute-start.7 = (bf16[1536,128]{1,0:T(8,128)(2,1)S(1)}, bf16[1536,128]{1,0:T(8,128)(2,1)S(1)}, u32[]{:S(2)}, u32[]{:S(2)}) collective-permute-start(bf16[1536,128]{1,0:T(8,128)(2,1)S(1)} %maximum_maximum_fusion), channel_id=1, source_target_pairs={{0,4},{4,0},{8,12},{12,8},{16,20},{20,16},{24,28},{28,24},{1,5},{5... | collective-permute-start | bytes 1179656 | tf_op jit(solution)/shard_map/ppermute | solution.py:150
  436.6 17.7 %collective-permute-start.8 = (bf16[1536,128]{1,0:T(8,128)(2,1)S(1)}, bf16[1536,128]{1,0:T(8,128)(2,1)S(1)}, u32[]{:S(2)}, u32[]{:S(2)}) collective-permute-start(bf16[1536,128]{1,0:T(8,128)(2,1)S(1)} %maximum_maximum_fusion.1), channel_id=1, source_target_pairs={{0,8},{4,12},{8,0},{12,4},{16,24},{20,28},{24,16},{28,20},{1,9},{5... | collective-permute-start | bytes 1179656 | tf_op jit(solution)/shard_map/ppermute | solution.py:150
  539.0 218.9 %reduce-scatter.9.cloned.1.call-start = ((), (), s32[]{:S(2)}) async-start(), calls=%async_computation.9 | async-start | bytes 4866048 | tf_op jit(solution)/shard_map/reduce_scatter | solution.py:158
  550.8 319.1 %reduce-scatter.11.cloned.1.call-start = ((), (), s32[]{:S(2)}) async-start(), calls=%async_computation.10 | async-start | bytes 4866048 | tf_op jit(solution)/shard_map/reduce_scatter | solution.py:158
  599.7 101.5 %collective-permute-start.10 = (bf16[1024,768]{0,1:T(8,128)(2,1)}, bf16[1024,768]{0,1:T(8,128)(2,1)S(1)}, u32[]{:S(2)}, u32[]{:S(2)}) collective-permute-start(bf16[1024,768]{0,1:T(8,128)(2,1)} %get-tuple-element.77), channel_id=1, source_target_pairs={{0,4},{4,0},{8,12},{12,8},{16,20},{20,16},{24,28},{28,24},{1,5},{5... | collective-permute-start | bytes 4718600 | tf_op jit(solution)/shard_map/ppermute | solution.py:150
  600.9 100.4 %collective-permute-start.11 = (bf16[1024,768]{0,1:T(8,128)(2,1)}, bf16[1024,768]{0,1:T(8,128)(2,1)}, u32[]{:S(2)}, u32[]{:S(2)}) collective-permute-start(bf16[1024,768]{0,1:T(8,128)(2,1)} %get-tuple-element.79), channel_id=1, source_target_pairs={{0,8},{4,12},{8,0},{12,4},{16,24},{20,28},{24,16},{28,20},{1,9},{5... | collective-permute-start | bytes 4718600 | tf_op jit(solution)/shard_map/ppermute | solution.py:150
  601.2 100.1 %collective-permute-start.12 = (bf16[1024,768]{0,1:T(8,128)(2,1)}, bf16[1024,768]{0,1:T(8,128)(2,1)}, u32[]{:S(2)}, u32[]{:S(2)}) collective-permute-start(bf16[1024,768]{0,1:T(8,128)(2,1)} %get-tuple-element.78), channel_id=1, source_target_pairs={{0,12},{4,8},{8,4},{12,0},{16,28},{20,24},{24,20},{28,16},{1,13},{... | collective-permute-start | bytes 4718600 | tf_op jit(solution)/shard_map/ppermute | solution.py:150
  (66 other events, 452.0 us)
Sparse Core Ops, SparseCore 0:
  10.9 57.1 all-gather.7
  71.0 64.7 all-gather.5
  138.7 65.3 all-gather.9
  206.9 61.9 all-gather.11
  434.2 94.2 reduce-scatter.6
  539.2 106.7 reduce-scatter.12
  651.4 106.5 reduce-scatter.8
  763.5 106.4 reduce-scatter.10

commit v2 on v1

--- a/solution.py
+++ b/solution.py
@@ -1,3 +1,4 @@
+import functools
 import jax
 import jax.numpy as jnp
 from jax import lax
@@ -145,6 +146,300 @@
       scratch_shapes=[pltpu.VMEM((2*n,128),F32),pltpu.VMEM((n,128),F32),pltpu.VMEM((2*n,128),F32)],
       compiler_params=pltpu.CompilerParams(vmem_limit_bytes=VMEM_ALL),name="att_bwd")(pos,left,right,g)
 
+MESH = pl.DeviceIdType.MESH
+
+
+def bits_of(size):
+    return size.bit_length() - 1
+
+
+def steps_of(nt, ng):
+    return [("tok", b) for b in reversed(range(bits_of(nt)))] + [
+        ("grp", b) for b in reversed(range(bits_of(ng)))
+    ]
+
+
+def greet(peers):
+    barrier = pltpu.get_barrier_semaphore()
+    for peer in peers:
+        pl.semaphore_signal(barrier, inc=1, device_id=peer, device_id_type=MESH)
+    pl.semaphore_wait(barrier, len(peers))
+
+
+def collect_kernel(nt, ng, parts, *refs):
+    tok_in, pos_in, pin_in = refs[:3]
+    nf = (len(refs) - 13) // 2
+    full_in = refs[3:3 + nf]
+    tok_out, pos_out, pin_out = refs[3 + nf:6 + nf]
+    full_out = refs[6 + nf:6 + 2 * nf]
+    lsem, tsend, trecv, psend, precv, wsend, wrecv = refs[6 + 2 * nf:]
+    t = lax.axis_index("tok")
+    g = lax.axis_index("grp")
+    steps = steps_of(nt, ng)
+    nb = len(steps)
+    me = t * ng + g
+    digits = [(me // (1 << (nb - 1 - j))) % 2 for j in range(nb)]
+
+    def held_at(s):
+        return (slice(None),) * s + tuple(digits[s:])
+
+    def peer(axis, mask):
+        return {"tok": t ^ mask, "grp": g} if axis == "tok" else {"tok": t, "grp": g ^ mask}
+
+    count = tok_in.shape[0]
+    own = [pltpu.make_async_copy(tok_in, tok_out.at[0], lsem.at[0]),
+           pltpu.make_async_copy(pos_in.at[t % 4], pos_out.at[0], lsem.at[1])]
+    for i, (a, b) in enumerate(zip(full_in, full_out)):
+        own.append(pltpu.make_async_copy(a, b.at[held_at(0)], lsem.at[2 + i]))
+    greet([peer(axis, 1 << b) for axis, b in steps] + [peer("tok", 3)])
+    for copy in own:
+        copy.start()
+
+    flights = {}
+
+    def send(name, src, dst, sems, to):
+        copy = pltpu.make_async_remote_copy(
+            src_ref=src, dst_ref=dst, send_sem=sems[0], recv_sem=sems[1],
+            device_id=to, device_id_type=MESH)
+        copy.start()
+        flights[name] = copy
+
+    arrived = set()
+
+    def wait(name):
+        if name not in arrived:
+            arrived.add(name)
+            flights[name].wait_recv()
+
+    chunk = count // parts
+
+    def rows(c):
+        return pl.ds(c * chunk, chunk)
+
+    def token(c, mask):
+        i = (mask - 1) * parts + c
+        send(("t", mask, c), tok_in.at[rows(c)], tok_out.at[mask, rows(c)],
+             (tsend.at[i], trecv.at[i]), peer("tok", mask))
+
+    def relay(c):
+        i = 2 * parts + c
+        mask = 2 if c >= parts // 2 else 1
+        wait(("t", 3 - mask, c))
+        send(("r", c), tok_out.at[3 - mask, rows(c)], tok_out.at[3, rows(c)],
+             (tsend.at[i], trecv.at[i]), peer("tok", mask))
+
+    def position(mask):
+        i = mask - 1
+        send(("p", mask), pos_in.at[(t ^ mask) % 4], pos_out.at[mask],
+             (psend.at[i], precv.at[i]), peer("tok", mask))
+
+    def full(w, s):
+        axis, b = steps[s]
+        i = w * nb + s
+        to = peer(axis, 1 << b)
+        out = full_out[w]
+        if s == 0:
+            src, dst = full_in[w], out.at[held_at(0)]
+        else:
+            wait(("w", w, s - 1))
+            if s == 1:
+                own[2 + w].wait()
+            src = out.at[held_at(s)]
+            dst = src
+        send(("w", w, s), src, dst, (wsend.at[i], wrecv.at[i]), to)
+
+    def slices(s):
+        axis, b = steps[s]
+        i = nf * nb + s
+        to = peer(axis, 1 << b)
+        tb = bits_of(nt)
+        if s > 0:
+            wait(("w", nf, s - 1))
+        high = tb - 2
+        theirs = (t ^ (1 << b)) if axis == "tok" else t
+        if s < high:
+            place = (slice(None), slice(None))
+        elif s == high:
+            place = ((theirs // 2) % 2, slice(None))
+        else:
+            place = ((theirs // 2) % 2, theirs % 2)
+        src = pin_out.at[place + held_at(s)]
+        send(("w", nf, s), src, src, (wsend.at[i], wrecv.at[i]), to)
+
+    pin_own = pltpu.make_async_copy(pin_in, pin_out.at[(slice(None), slice(None)) + held_at(0)], lsem.at[2 + nf])
+    pin_own.start()
+    order = list(range(nf))
+    half = parts // 2
+    for c in range(half):
+        token(c, 1)
+    for w in order:
+        full(w, 0)
+    pin_own.wait()
+    slices(0)
+    for mask in (1, 2, 3):
+        position(mask)
+    token(0, 2)
+    done_y, done_z = half, 1
+    for s in range(1, nb):
+        for w in order:
+            full(w, s)
+            if w >= 0:
+                if done_z < parts:
+                    token(done_z, 2)
+                    done_z += 1
+                if done_y < parts and s >= 2:
+                    token(done_y, 1)
+                    done_y += 1
+        slices(s)
+        if s == nb - 2:
+            for c in range(done_z, parts):
+                token(c, 2)
+            for c in range(done_y, parts):
+                token(c, 1)
+            for c in range(parts):
+                relay(c)
+    own[0].wait()
+    own[1].wait()
+    if nb == 1:
+        for w in range(nf):
+            own[2 + w].wait()
+    for name in flights:
+        wait(name)
+    for copy in flights.values():
+        copy.wait_send()
+
+
+def collect(nt, ng, tokens, pos, pin, fulls, parts=4):
+    n = nt * ng
+    nb = bits_of(nt) + bits_of(ng)
+    hbm = pl.BlockSpec(memory_space=pl.ANY)
+    vm = pl.BlockSpec(memory_space=pltpu.VMEM)
+    S = jax.ShapeDtypeStruct
+    block, at, own, *wide = pl.pallas_call(
+        functools.partial(collect_kernel, nt, ng, parts),
+        out_shape=[S((4,) + tokens.shape, tokens.dtype), S((4,) + pos.shape[1:], pos.dtype),
+                   S((2, 2) + (2,) * nb + pin.shape[1:], pin.dtype)] + [S((2,) * nb + f.shape, f.dtype) for f in fulls],
+        in_specs=[vm] * (3 + len(fulls)),
+        out_specs=[hbm] * (3 + len(fulls)),
+        scratch_shapes=[
+            pltpu.SemaphoreType.DMA((3 + len(fulls),)),
+            pltpu.SemaphoreType.DMA((3 * parts,)), pltpu.SemaphoreType.DMA((3 * parts,)),
+            pltpu.SemaphoreType.DMA((3,)), pltpu.SemaphoreType.DMA((3,)),
+            pltpu.SemaphoreType.DMA(((len(fulls) + 1) * nb,)), pltpu.SemaphoreType.DMA(((len(fulls) + 1) * nb,)),
+        ],
+        compiler_params=pltpu.CompilerParams(collective_id=0, has_side_effects=True),
+        name="collect",
+    )(tokens, pos, pin.reshape((2, 2) + pin.shape[1:]), *fulls)
+    return [block, at, own.reshape((4, n) + pin.shape[1:])] + [
+        w.reshape((n,) + f.shape) for w, f in zip(wide, fulls)]
+
+
+def reduce_kernel(nt, ng, *refs):
+    pin_in, pout_in, small_in, pin_out, pout_out, small_out = refs[:6]
+    nb = bits_of(nt) + bits_of(ng)
+    tb = bits_of(nt)
+    pin_a, pout_a, small_a, quad = refs[6:10]
+    landing = refs[10:10 + 3 * nb]
+    ssem, rsem = refs[10 + 3 * nb:]
+    t = lax.axis_index("tok")
+    g = lax.axis_index("grp")
+    steps = steps_of(nt, ng)
+    me = t * ng + g
+    digits = [(me // (1 << (nb - 1 - j))) % 2 for j in range(nb)]
+
+    def peer(s):
+        axis, b = steps[s]
+        mask = 1 << b
+        return {"tok": t ^ mask, "grp": g} if axis == "tok" else {"tok": t, "grp": g ^ mask}
+
+    greet([peer(s) for s in range(nb)])
+    p1, p0 = (t // 2) % 2, t % 2
+    flying = []
+
+    def launch(i, src, dst, s):
+        copy = pltpu.make_async_remote_copy(
+            src_ref=src, dst_ref=dst, send_sem=ssem.at[i], recv_sem=rsem.at[i],
+            device_id=peer(s), device_id_type=MESH)
+        copy.start()
+        flying.append(copy)
+        return copy
+
+    def away(s):
+        return (slice(None),) * s + (1 - digits[s],) + tuple(digits[s + 1:])
+
+    def kept(s):
+        return (slice(None),) * s + tuple(digits[s:])
+
+    def add(ref, at, other, dst, to):
+        value = ref[at].astype(F32) + other[...].astype(F32)
+        dst[to] = value.astype(dst.dtype)
+
+    for s in reversed(range(nb)):
+        first = s == nb - 1
+        outer = s >= tb
+        sources = [pin_in if first else pin_a, pout_in if first else pout_a, small_in if first else small_a]
+        copies = []
+        for w in range(3):
+            land = landing[w * nb + s]
+            i = w * nb + s
+            if w == 0 and not outer:
+                place = {tb - 1: (p1, p0), tb - 2: (p1, slice(None))}.get(s, (slice(None), slice(None)))
+                cut = (slice(None),) * s + (1 - digits[s],) + tuple(digits[s + 1:tb])
+                src = quad.at[place + cut]
+                copies.append(launch(i, src, src if s >= tb - 2 else land, s))
+            else:
+                copies.append(launch(i, sources[w].at[away(s)], land, s))
+        for w in range(3):
+            copies[w].wait_recv()
+            land = landing[w * nb + s]
+            if w == 0 and not outer:
+                if s < tb - 2:
+                    at = (slice(None), slice(None)) + (slice(None),) * s + tuple(digits[s:tb])
+                    add(quad, at, land, quad, at)
+            elif w == 0 and s == tb:
+                add(sources[0], kept(s), land, quad, (p1, p0))
+            else:
+                dst = (pin_a, pout_a, small_a)[w]
+                add(sources[w], kept(s), land, dst, kept(s))
+    for copy in flying:
+        copy.wait_send()
+    pin_out[...] = quad[(slice(None), slice(None)) + tuple(digits[:tb])]
+    pout_out[...] = pout_a[tuple(digits)]
+    small_out[...] = small_a[tuple(digits)]
+
+
+def reduce_small(nt, ng, pin, pout, small):
+    nb = bits_of(nt) + bits_of(ng)
+    tb = bits_of(nt)
+    two = (2,) * nb
+    r, c = pin.shape[1:]
+    rp = pout.shape[1:]
+    rs = small.shape[1:]
+    S = jax.ShapeDtypeStruct
+    vm = pl.BlockSpec(memory_space=pltpu.VMEM)
+    landing = []
+    for w, (shape, dt) in enumerate((((r, c), BF), (rp, BF), (rs, F32))):
+        for s in range(nb):
+            lead = (2,) * s
+            if w == 0 and s < tb:
+                lead = ((2, 2) + lead) if s < tb - 2 else (1,)
+                landing.append(pltpu.VMEM(lead + (shape if s < tb - 2 else (8, 128)), dt))
+            else:
+                landing.append(pltpu.VMEM(lead + shape, dt))
+    return pl.pallas_call(
+        functools.partial(reduce_kernel, nt, ng),
+        out_shape=[S((2, 2, r, c), BF), S(rp, BF), S(rs, F32)],
+        in_specs=[vm] * 3,
+        out_specs=[vm] * 3,
+        scratch_shapes=[
+            pltpu.VMEM(two + (r, c), BF), pltpu.VMEM(two + rp, BF), pltpu.VMEM(two + rs, F32),
+            pltpu.VMEM((2, 2) + (2,) * tb + (r, c), BF),
+        ] + landing + [pltpu.SemaphoreType.DMA((3 * nb,)), pltpu.SemaphoreType.DMA((3 * nb,))],
+        compiler_params=pltpu.CompilerParams(collective_id=1, has_side_effects=True, vmem_limit_bytes=VMEM_ALL),
+        name="reduce_small",
+    )(pin.reshape(two + (r, c)), pout.reshape(two + rp), small.reshape(two + rs))
+
+
 def flip(block, mask):
     count = lax.axis_size("tok")
     return lax.ppermute(block, "tok", [(i, i ^ mask) for i in range(count)])
@@ -186,40 +481,48 @@
     offset = lax.axis_index("tok") % span
     total = span * count
 
-    near = flip(inputs, 1)
-    far = flip(jnp.stack([inputs, near]), 2)
-    block = jnp.concatenate([inputs[None], near[None], far]).reshape(total, width)
-    near_at = flip(positions, 1)
-    far_at = flip(jnp.stack([positions, near_at]), 2)
-    block_at = jnp.concatenate([positions[None], near_at[None], far_at])
-    own_at = lax.dynamic_slice_in_dim(block_at, offset * mine, mine, axis=1)
-    own_at = own_at.transpose(1, 0, 2).reshape(-1)
-
-    project_in = gather_all(project_in)
-    project_out = gather_all(project_out)
-    expand = gather_all(expand)
-    contract = gather_all(contract)
+    nt = lax.axis_size("tok")
+    ng = lax.axis_size("grp")
+    devices = nt * ng
+    few = query_bias.shape[0]
+    strips = expand.shape[1] // width
+
+    wide = jnp.concatenate(
+        [expand.reshape(few, strips, width).transpose(1, 0, 2).reshape(-1, width), contract], axis=0
+    )
+    wide = gather_all(wide[None])
+    expand = wide[:, : strips * few].reshape(devices, strips, few, width)
+    expand = expand.transpose(0, 2, 1, 3).reshape(width, strips * width)
+    contract = wide[:, strips * few :].reshape(strips * width, width)
+
+    pieces = project_in.reshape(few, 3, span, mine, head_dim)
+    hollow = jnp.zeros((few, head_dim), BF)
+    arranged = []
+    for place in range(span):
+        columns = []
+        for h in range(mine):
+            query, key, value = (pieces[:, i, place, h] for i in range(3))
+            columns += [hollow, query, value, key] if h == 0 else [query, hollow, key, value]
+        arranged.append(jnp.concatenate(columns, axis=1))
     packed = jnp.concatenate(
         [
             query_bias, value_bias, output_bias, first_gain, first_shift,
             contract_bias, second_gain, second_shift, expand_bias,
         ]
-    )
-    few = query_bias.shape[0]
-    packed = gather_all(packed[None].astype(F32))
+    ).astype(F32)
+    packed = jnp.pad(packed, (0, 1024 - packed.shape[0])).reshape(8, 128)
+    block, own_at, arranged, packed, project_out = collect(
+        nt, ng, inputs, positions.reshape(span, mine, count), jnp.stack(arranged), [packed, project_out]
+    )
+    block = block.reshape(total, width)
+    own_at = own_at.transpose(1, 0, 2).reshape(-1)
+    arranged = lax.dynamic_index_in_dim(arranged, offset, 0, False).reshape(width, -1)
+    project_out = project_out.reshape(width, width)
+    packed = packed.reshape(devices, -1)
     vectors = [packed[:, i * few : (i + 1) * few].reshape(-1) for i in range(8)]
     query_bias, value_bias, output_bias, gain_one, shift_one, contract_bias, gain_two, shift_two = vectors
-    expand_bias = packed[:, 8 * few :].reshape(-1)
-
-    pieces = lax.dynamic_slice_in_dim(
-        project_in.reshape(width, 3, heads, head_dim), offset * mine, mine, axis=2
-    )
-    hollow = jnp.zeros((width, head_dim), BF)
-    columns = []
-    for h in range(mine):
-        query, key, value = pieces[:, 0, h], pieces[:, 1, h], pieces[:, 2, h]
-        columns += [hollow, query, value, key] if h == 0 else [query, hollow, key, value]
-    arranged = jnp.concatenate(columns, axis=1)
+    expand_bias = packed[:, 8 * few : (8 + strips) * few].reshape(-1)
+
     own_query = lax.dynamic_slice_in_dim(query_bias.reshape(heads, head_dim), offset * mine, mine)
     own_value = lax.dynamic_slice_in_dim(value_bias.reshape(heads, head_dim), offset * mine, mine)
     blank = jnp.zeros((head_dim,), F32)
@@ -292,6 +595,17 @@
         one = jnp.concatenate([one[: count // 2], one[count // 2 :]], axis=1)
         sending.append(jnp.concatenate([two, one], axis=0))
     landed = [sending[0]] + [flip(sending[k], k) for k in range(1, span)]
+    expand_grad = expand_grad.astype(BF)
+    contract_grad = contract_grad.astype(BF)
+    landed, expand_grad, contract_grad = lax.optimization_barrier((landed, expand_grad, contract_grad))
+    wide_grad = jnp.concatenate(
+        [expand_grad[:, i * width : (i + 1) * width].reshape(devices, few, width) for i in range(strips)]
+        + [contract_grad.reshape(devices, strips * few, width)],
+        axis=1,
+    )
+    wide_grad = scatter_sum(wide_grad)[0].astype(F32)
+    expand_grad = wide_grad[: strips * few].reshape(strips, few, width).transpose(1, 0, 2).reshape(few, -1)
+    contract_grad = wide_grad[strips * few :]
     grad_pair = jnp.concatenate([item[:count] for item in landed], axis=0)
     grad_single = jnp.concatenate([open_single(item[count:]) for item in landed], axis=0)
     grad_att = jnp.stack([grad_pair, jnp.concatenate([grad_single, grad_single], axis=1)])
@@ -300,7 +614,7 @@
     arranged_grad = jnp.concatenate(
         [jnp.einsum("rd,re->de", block, grad_rows[h], preferred_element_type=F32) for h in range(mine)],
         axis=1,
-    ).reshape(width, mine, 4, head_dim)
+    ).astype(BF)
     sums = jnp.sum(grad_rows.astype(F32), axis=1).reshape(mine, 4, head_dim)
     query_at = [1] + [0] * (mine - 1)
     key_at = [3] + [2] * (mine - 1)
@@ -309,12 +623,6 @@
     def spread(take, at):
         return jnp.stack([take(h, at[h]) for h in range(mine)], axis=-2)
 
-    own_grad = jnp.stack(
-        [spread(lambda h, s: arranged_grad[:, h, s], at) for at in (query_at, key_at, value_at)], axis=1
-    )
-    project_in_grad = lax.dynamic_update_slice_in_dim(
-        jnp.zeros((width, 3, heads, head_dim), F32), own_grad, offset * mine, axis=2
-    ).reshape(width, 3 * width)
     own_sums = jnp.stack([spread(lambda h, s: sums[h, s], at) for at in (query_at, value_at)])
     bias_grads = lax.dynamic_update_slice_in_dim(
         jnp.zeros((2, heads, head_dim), F32), own_sums, offset * mine, axis=1
@@ -339,11 +647,6 @@
     project_out_grad = jnp.concatenate(
         [lax.dynamic_index_in_dim(by_owner, offset ^ k, 0, False) for k in range(span)], axis=0
     )
-    project_in_grad = scatter_sum(project_in_grad.astype(BF)).astype(F32)
-    project_out_grad = scatter_sum(project_out_grad.astype(BF)).astype(F32)
-    expand_grad = scatter_sum(expand_grad.astype(BF)).astype(F32)
-    contract_grad = scatter_sum(contract_grad.astype(BF)).astype(F32)
-    devices = lax.axis_size("tok") * lax.axis_size("grp")
     small = jnp.concatenate(
         [
             item.reshape(devices, -1)
@@ -354,8 +657,24 @@
         ],
         axis=1,
     )
-    small = scatter_sum(small)[0]
-    each = [small[i * few : (i + 1) * few] for i in range(8)] + [small[8 * few :]]
+    small = jnp.pad(small, ((0, 0), (0, 1024 - small.shape[1]))).reshape(devices, 8, 128)
+    project_in_grad, project_out_grad, small = reduce_small(
+        nt, ng, arranged_grad.reshape(devices, few, -1),
+        project_out_grad.astype(BF).reshape(devices, few, width), small,
+    )
+    project_in_grad = project_in_grad.astype(F32).reshape(span, few, mine, 4, head_dim)
+    project_in_grad = jnp.concatenate(
+        [
+            project_in_grad[place, :, h, at[h]]
+            for at in (query_at, key_at, value_at)
+            for place in range(span)
+            for h in range(mine)
+        ],
+        axis=1,
+    )
+    project_out_grad = project_out_grad.astype(F32)
+    small = small.reshape(-1)
+    each = [small[i * few : (i + 1) * few] for i in range(8)] + [small[8 * few : (8 + strips) * few]]
     return (
         result.astype(BF)[None],
         token_grad[None],

time: 894 us -> 663 us (0.74)
  waiting for transfers between devices: 232 us -> 7.3 us
  blocking collectives: 208 us -> 0 us
  Pallas kernels: 139 us -> 334 us
  local copies, waits for them, and re-layouts: 89.6 us -> 115 us
    pallas_call x0 -> x2, Pallas kernels: none -> 195 us  [the longest x1 114 us: collect(): pl.pallas_call(functools.partial(collect_kernel, nt, ng, parts), out_shap...]
    reduce_scatter x3 -> x1, waiting for transfers between devices: 156 us -> 0.01 us  [scatter_sum(): lax.psum_scatter(item, ('tok', 'grp'), scatter_dimension=0, tiled=True)]
    all_gather x1 -> x0, blocking collectives: 120 us -> none  [gather_all(): return lax.all_gather(item, ('tok', 'grp'), axis=0, tiled=True)]
    unnamed x1 -> x0, blocking collectives: 88.7 us -> none
    ppermute x13 -> x9, waiting for transfers between devices: 73.7 us -> 7.25 us  [flip(): return lax.ppermute(block, 'tok', [(i, i ^ mask) for i in range(count)])]
    unnamed x169 -> x137, local copies, waits for them, and re-layouts: 45.3 us -> 28.4 us
    slice x4 -> x11, local copies, waits for them, and re-layouts: 2.2 us -> 15.4 us  [the longest x1 6.53 us: shards(): contract = wide[:, strips * few:].reshape(strips * width, width)]
  transfers between devices with their start and end apart: 21 -> 11, of which waited for: 8 -> 2; matrix products, arithmetic and copies ran while one was open for 24% -> 24% of each run, Pallas kernels for 16% -> 51%
where the time goes in v2:
time: 663 us; the launch traced here: 653 us
  Pallas kernels  334 us (50%)
  matrix products  135 us (20%)
  local copies, waits for them, and re-layouts  115 us (17%)
  other arithmetic  35.6 us (5%)
  between operations  15.5 us (2%)
  starting transfers between devices  10.5 us (2%)
  waiting for transfers between devices  7.3 us (1%)
    pallas_call x1, Pallas kernels, collect(): pl.pallas_call(functools.partial(collect_kernel, nt, ng, parts), out_shap...  114 us
    pallas_call x1, Pallas kernels, reduce_small(): pl.pallas_call(functools.partial(reduce_kernel, nt, ng), out_shape=[S((2,...  81.3 us
    pallas_call x1, Pallas kernels, fwd(): pl.pallas_call(fwd_kernel, grid=(H,), out_shape=(jax.ShapeDtypeStruct((H,...  73.7 us
    pallas_call x1, Pallas kernels, bwd(): pl.pallas_call(bwd_kernel, grid=(H,), out_shape=jax.ShapeDtypeStruct((H,...  65.6 us
    dot_general x1, matrix products, shards(): jnp.dot(normed_low, expand, preferred_element_type=F32) + expand_bias  36.6 us
    dot_general x3, matrix products, shards(): jnp.einsum('re,de->rd', grad_rows[h], arranged[:, 256 * h:256 * h + 256],...  32.5 us
    unnamed x137, local copies, waits for them, and re-layouts  28.4 us
  transfers between devices with their start and end apart: 11, of which 2 were waited for; matrix products, arithmetic and copies ran while one was open for 24% of the time, Pallas kernels for 51%

profile of v2, /device:TPU:0, one launch (start us, length us, event | category | flops | bytes accessed | tf_op | source)
XLA Modules:
  0.0 652.9 jit_solution(11036372498949849057)
XLA Ops:
  15.3 113.7 %collect.1 = (bf16[4,1024,768]{2,1,0:T(8,128)(2,1)}, s32[4,3,1024]{2,1,0:T(4,128)}, bf16[2,2,2,2,2,2,2,24,768]{8,7,6,5,4,3,2,1,0:T(8,128)(2,1)}, f32[2,2,2,2,2,8...) custom-call(bf16[1024,768]{1,0:T(8,128)(2,1)} %bitcast.324, s32[4,3,1024]{2,1,0:T(4,128)} %add_select_fusion.refs_1_, ...), custom_call_target="tpu_custom_call" | custom-call | tf_op jit(solution)/shard_map/collect/pallas_call | solution.py:318
  136.2 73.7 %att_fwd.1 = (bf16[3,4096,128]{2,1,0:T(8,128)(2,1)}, bf16[3,4096,128]{2,1,0:T(8,128)(2,1)}, bf16[3,4096,128]{2,1,0:T(8,128)(2,1)}) custom-call(s32[12288]{0:T(1024)} %bitcast.367, bf16[4096,768]{1,0:T(8,128)(2,1)} %bitcast.310, bf16[768,768]{1,0:T(8,128)(2,1)} %bitcast.314, f32[3,1,256]{2,1,0:T(1,128)} %broadcast_in_dim.36.bias), custom_call_target="tpu_custom_call" | custom-call | tf_op jit(solution)/shard_map/att_fwd/pallas_call | solution.py:82
  244.7 8.8 %copy.2123 = bf16[768,4096]{1,0:T(8,128)(2,1)} copy(bf16[768,4096]{0,1:T(8,128)(2,1)} %bitcast.311) | data formatting | bytes 12582912 | tf_op jit(solution)/shard_map/rd,re->de/dot_general | solution.py:615
  266.7 3.8 concatenate.115
  270.5 3.9 fusion.98
  276.4 6.5 fusion.81
  287.2 36.6 %fusion.2 = (bf16[1024,3072]{1,0:T(8,128)(2,1)}, f32[1024,3072]{1,0:T(8,128)}) fusion(f32[3072]{0:T(1024)S(1)} %copy-done.25, bf16[768,3072]{1,0:T(8,128)(2,1)S(1)} %bitcast.335, f32[1024,768]{0,1:T(8,128)S(1)} %copy-done.2, f32[768]{0:T(1024)S(1)} %copy-done.26, f32[768]{0:T(1024)S(1)} %mul.139, f32[1024]{0:T(1024)S(1)} %add_rsqrt_fusion.1, ...), kind=kOutput, calls=%fused_computation.4 | convolution fusion | flops 5043388416 | bytes 26765312 | tf_op jit(solution)/shard_map/dot_general | solution.py:558
  323.8 9.0 %fusion.99 = (f32[1024]{0:T(1024)S(1)}, f32[1024,768]{0,1:T(8,128)S(1)}) fusion(f32[768]{0:T(1024)S(1)} %copy-done.27, bf16[1024,3072]{1,0:T(8,128)(2,1)} %get-tuple-element.205, bf16[3072,768]{1,0:T(8,128)(2,1)} %bitcast.338, f32[768]{0:T(1024)S(1)} %copy-done.26, f32[768]{0:T(1024)S(1)} %mul.139, f32[1024]{0:T(1024)S(1)} %add_rsqrt_fusion.1, ...), kind=kOutput, calls=%fused_computation.253 | convolution fusion | flops 4837342208 | bytes 17323008 | tf_op jit(solution)/shard_map/dot_general | solution.py:560
  334.3 3.1 convert_reduce_fusion.3
  337.4 9.9 %convolution_convert_fusion = bf16[3072,768]{1,0:T(8,128)(2,1)} fusion(bf16[1024,3072]{1,0:T(8,128)(2,1)} %get-tuple-element.205, f32[1024,768]{0,1:T(8,128)S(1)} %get-tuple-element.57), kind=kOutput, calls=%fused_computation.29 | convolution fusion | flops 4834983936 | bytes 14155776 | tf_op jit(solution)/shard_map/rf,rd->fd/dot_general | solution.py:568
  347.3 13.1 %convert_reduce_fusion = (f32[3072]{0:T(1024)S(1)}, bf16[1024,3072]{1,0:T(8,128)(2,1)}) fusion(f32[1024,3072]{1,0:T(8,128)} %get-tuple-element.206, f32[3072]{0:T(1024)S(1)} %copy-done.25, bf16[3072,768]{1,0:T(8,128)(2,1)S(1)} %bitcast.341, f32[1024,768]{0,1:T(8,128)S(1)} %get-tuple-element.57), kind=kOutput, calls=%fused_computation.11 | convolution fusion | flops 4873516032 | bytes 26763264 | tf_op jit(solution)/shard_map/rd,fd->rf/dot_general | solution.py:569
  360.4 10.1 %convolution_convert_fusion.1 = bf16[768,3072]{1,0:T(8,128)(2,1)} fusion(bf16[1024,3072]{1,0:T(8,128)(2,1)} %get-tuple-element.213, f32[1024,768]{0,1:T(8,128)S(1)} %copy-done.2, f32[768]{0:T(1024)S(1)} %copy-done.26, f32[768]{0:T(1024)S(1)} %mul.139, f32[1024]{0:T(1024)S(1)} %add_rsqrt_fusion.1, f32[1024]{0:T(1024)S(1)} %broadcast_multiply_fusion.5), kind=kOutput, calls=%fused_computation.30 | convolution fusion | flops 4838129664 | bytes 14170112 | tf_op jit(solution)/shard_map/rd,rf->df/dot_general | solution.py:576
  370.5 6.0 multiply_reduce_fusion.1
  377.6 3.5 convolution_convert_fusion.2
  395.3 6.3 collective-permute-done.4
  425.0 65.6 %att_bwd.1 = bf16[3,4096,256]{2,1,0:T(8,128)(2,1)} custom-call(s32[12288]{0:T(1024)} %bitcast.368, bf16[3,4096,128]{2,1,0:T(8,128)(2,1)} %get-tuple-element.38.left, bf16[3,4096,128]{2,1,0:T(8,128)(2,1)} %get-tuple-element.39.right, bf16[2,4096,128]{2,1,0:T(8,128)(2,1)} %pad_maximum_fusion.g), custom_call_target="tpu_custom_call" | custom-call | tf_op jit(solution)/shard_map/att_bwd/pallas_call | solution.py:142
  490.6 3.9 convert_reduce_fusion.1
  495.9 8.5 %fusion.27 = f32[4096,768]{0,1:T(8,128)} fusion(bf16[3,4096,256]{2,1,0:T(8,128)(2,1)} %att_bwd.1, bf16[768,768]{1,0:T(8,128)(2,1)} %bitcast.315), kind=kOutput, calls=%fused_computation.72 | convolution fusion | flops 1610612736 | bytes 15073280 | tf_op jit(solution)/shard_map/re,de->rd/dot_general | solution.py:631
  504.3 7.4 %fusion.29 = f32[4096,768]{0,1:T(8,128)} fusion(bf16[3,4096,256]{2,1,0:T(8,128)(2,1)S(1)} %bitcast.309, bf16[768,768]{1,0:T(8,128)(2,1)} %bitcast.316), kind=kOutput, calls=%fused_computation.74 | convolution fusion | flops 1610612736 | bytes 15073280 | tf_op jit(solution)/shard_map/re,de->rd/dot_general | solution.py:631
  511.7 16.6 %fusion.100 = (bf16[4096,768]{0,1:T(8,128)(2,1)}, f32[4096,768]{0,1:T(8,128)}) fusion(bf16[768,768]{1,0:T(8,128)(2,1)} %bitcast.317, bf16[3,4096,256]{2,1,0:T(8,128)(2,1)S(1)} %bitcast.309, f32[4096,768]{0,1:T(8,128)} %fusion.29, f32[4096,768]{0,1:T(8,128)} %fusion.27), kind=kOutput, calls=%fused_computation.254 | convolution fusion | flops 1620049920 | bytes 46530560 | tf_op jit(solution)/shard_map/re,de->rd/dot_general | solution.py:631
  528.4 4.8 fusion.82
  536.7 4.8 fusion.37
  546.6 81.3 %reduce_small.1 = (bf16[2,2,24,768]{3,2,1,0:T(8,128)(2,1)}, bf16[24,768]{1,0:T(8,128)(2,1)}, f32[8,128]{1,0:T(8,128)}) custom-call(bf16[2,2,2,2,2,24,768]{6,5,4,3,2,1,0:T(8,128)(2,1)} %pad_maximum_fusion.1.refs_0_, bf16[2,2,2,2,2,24,768]{6,5,4,3,2,1,0:T(8,128)(2,1)} %bitcast.337, f32[2,2,2,2,2,8,128]{6,5,4,3,2,1,0:T(8,128)} %bitcast.365), custom_call_target="tpu_custom_call" | custom-call | tf_op jit(solution)/shard_map/reduce_small/pallas_call | solution.py:429
  634.6 5.5 fusion.18
  (302 shorter events, 131.1 us)
Async XLA Ops:
  7.3 269.2 %all-gather.3.cloned.1.call-start = ((), (), s32[]{:S(2)}) async-start(), calls=%async_computation.2 | async-start | bytes 9732096 | tf_op jit(solution)/shard_map/all_gather | solution.py:449
  10.0 632.4 %reduce-scatter.2.cloned.1.call-start = ((), (), s32[]{:S(2)}) async-start(), calls=%async_computation.1 | async-start | bytes 9732096 | tf_op jit(solution)/shard_map/reduce_scatter | solution.py:453
  215.7 15.8 %copy-start.4 = (bf16[1,1024,768]{2,1,0:T(8,128)(2,1)S(1)}, bf16[1,1024,768]{2,1,0:T(8,128)(2,1)}, u32[]{:S(2)}) copy-start(bf16[1,1024,768]{2,1,0:T(8,128)(2,1)} %param.17) | copy-start | bytes 4718596
  216.7 42.7 %collective-permute-start.2 = (bf16[1536,128]{1,0:T(8,128)(2,1)}, bf16[1536,128]{1,0:T(8,128)(2,1)}, u32[]{:S(2)}, u32[]{:S(2)}) collective-permute-start(bf16[1536,128]{1,0:T(8,128)(2,1)} %get-tuple-element.84), channel_id=1, source_target_pairs={{0,12},{4,8},{8,4},{12,0},{16,28},{20,24},{24,20},{28,16},{1,13},{... | collective-permute-start | bytes 1179656 | tf_op jit(solution)/shard_map/ppermute | solution.py:445
  217.0 40.8 %collective-permute-start.1 = (bf16[1536,128]{1,0:T(8,128)(2,1)}, bf16[1536,128]{1,0:T(8,128)(2,1)}, u32[]{:S(2)}, u32[]{:S(2)}) collective-permute-start(bf16[1536,128]{1,0:T(8,128)(2,1)} %get-tuple-element.85), channel_id=1, source_target_pairs={{0,8},{4,12},{8,0},{12,4},{16,24},{20,28},{24,16},{28,20},{1,9},{5... | collective-permute-start | bytes 1179656 | tf_op jit(solution)/shard_map/ppermute | solution.py:445
  219.5 36.6 %collective-permute-start = (bf16[1536,128]{1,0:T(8,128)(2,1)}, bf16[1536,128]{1,0:T(8,128)(2,1)}, u32[]{:S(2)}, u32[]{:S(2)}) collective-permute-start(bf16[1536,128]{1,0:T(8,128)(2,1)} %get-tuple-element.86), channel_id=1, source_target_pairs={{0,4},{4,0},{8,12},{12,8},{16,20},{20,16},{24,28},{28,24},{1,5},{5... | collective-permute-start | bytes 1179656 | tf_op jit(solution)/shard_map/ppermute | solution.py:445
  231.8 8.2 %copy-start.15 = (f32[32,24]{1,0:T(8,128)S(1)}, f32[32,24]{1,0:T(8,128)}, u32[]{:S(2)}) copy-start(f32[32,24]{1,0:T(8,128)} %get-tuple-element.173) | copy-start | bytes 9220
  231.8 8.9 %copy-start.14 = (f32[32,24]{1,0:T(8,128)S(1)}, f32[32,24]{1,0:T(8,128)}, u32[]{:S(2)}) copy-start(f32[32,24]{1,0:T(8,128)} %get-tuple-element.171) | copy-start | bytes 9220
  231.8 9.6 %copy-start.13 = (f32[32,24]{1,0:T(8,128)S(1)}, f32[32,24]{1,0:T(8,128)}, u32[]{:S(2)}) copy-start(f32[32,24]{1,0:T(8,128)} %get-tuple-element.169) | copy-start | bytes 9220
  262.2 8.2 %copy-start.28 = (f32[768]{0:T(1024)S(1)}, f32[768]{0:T(1024)}, u32[]{:S(2)}) copy-start(f32[768]{0:T(1024)} %add.148) | copy-start | bytes 9220
  287.2 36.6 %copy-start.27 = (f32[768]{0:T(1024)S(1)}, f32[768]{0:T(1024)}, u32[]{:S(2)}) copy-start(f32[768]{0:T(1024)} %add.160) | copy-start | bytes 9220
  334.3 13.0 %slice-start.6 = ((s8[4718592]{0:T(1024)(128)(4,1)}), s8[4194304]{0:T(1024)(128)(4,1)S(1)}, s32[]{:S(2)}) async-start(s8[4718592]{0:T(1024)(128)(4,1)} %bitcast.339), calls=%async_computation.9 | async-start | bytes 8388608
  337.4 9.9 %slice-start.7 = ((s8[4718592]{0:T(1024)(128)(4,1)}), s8[524288]{0:T(1024)(128)(4,1)S(1)}, s32[]{:S(2)}) async-start(s8[4718592]{0:T(1024)(128)(4,1)} %bitcast.339), calls=%async_computation.10 | async-start | bytes 1048576
  360.4 10.1 %copy-start.38 = (bf16[1024,3072]{1,0:T(8,128)(2,1)S(1)}, bf16[1024,3072]{1,0:T(8,128)(2,1)}, u32[]{:S(2)}) copy-start(bf16[1024,3072]{1,0:T(8,128)(2,1)} %get-tuple-element.213) | copy-start | bytes 18874372
  377.6 9.5 %copy-start = (f32[1024,768]{0,1:T(8,128)}, f32[1024,768]{0,1:T(8,128)S(1)}, u32[]{:S(2)}) copy-start(f32[1024,768]{0,1:T(8,128)S(1)} %get-tuple-element.59) | copy-start | bytes 9437188
  382.1 13.2 %collective-permute-start.5 = (bf16[1536,128]{0,1:T(8,128)(2,1)}, bf16[1536,128]{0,1:T(8,128)(2,1)}, u32[]{:S(2)}, u32[]{:S(2)}) collective-permute-start(bf16[1536,128]{0,1:T(8,128)(2,1)} %maximum_maximum_fusion.3), channel_id=1, source_target_pairs={{0,12},{4,8},{8,4},{12,0},{16,28},{20,24},{24,20},{28,16},{1,13},{... | collective-permute-start | bytes 1179656 | tf_op jit(solution)/shard_map/ppermute | solution.py:445
  383.6 18.0 %collective-permute-start.4 = (bf16[1536,128]{0,1:T(8,128)(2,1)}, bf16[1536,128]{0,1:T(8,128)(2,1)}, u32[]{:S(2)}, u32[]{:S(2)}) collective-permute-start(bf16[1536,128]{0,1:T(8,128)(2,1)} %maximum_maximum_fusion.2), channel_id=1, source_target_pairs={{0,8},{4,12},{8,0},{12,4},{16,24},{20,28},{24,16},{28,20},{1,9},{5... | collective-permute-start | bytes 1179656 | tf_op jit(solution)/shard_map/ppermute | solution.py:445
  386.5 15.1 %collective-permute-start.3 = (bf16[1536,128]{0,1:T(8,128)(2,1)}, bf16[1536,128]{0,1:T(8,128)(2,1)}, u32[]{:S(2)}, u32[]{:S(2)}) collective-permute-start(bf16[1536,128]{0,1:T(8,128)(2,1)} %maximum_maximum_fusion.1), channel_id=1, source_target_pairs={{0,4},{4,0},{8,12},{12,8},{16,20},{20,16},{24,28},{28,24},{1,5},{5... | collective-permute-start | bytes 1179656 | tf_op jit(solution)/shard_map/ppermute | solution.py:445
  495.2 9.2 %slice-start = ((s8[6291456]{0:T(1024)(128)(4,1)}), s8[4194304]{0:T(1024)(128)(4,1)S(1)}, s32[]{:S(2)}) async-start(s8[6291456]{0:T(1024)(128)(4,1)} %bitcast.308), calls=%async_computation.3 | async-start | bytes 8388608
  495.9 8.5 %slice-start.1 = ((s8[6291456]{0:T(1024)(128)(4,1)}), s8[2097152]{0:T(1024)(128)(4,1)S(1)}, s32[]{:S(2)}) async-start(s8[6291456]{0:T(1024)(128)(4,1)} %bitcast.308), calls=%async_computation.4 | async-start | bytes 4194304
  528.4 13.2 %slice-start.2 = ((s8[6291456]{0:T(1024)(128)(4,1)}), s8[2097152]{0:T(1024)(128)(4,1)S(1)}, s32[]{:S(2)}) async-start(s8[6291456]{0:T(1024)(128)(4,1)} %bitcast.320), calls=%async_computation.5 | async-start | bytes 4194304
  533.2 101.4 %collective-permute-start.6 = (bf16[1024,768]{0,1:T(8,128)(2,1)}, bf16[1024,768]{0,1:T(8,128)(2,1)}, u32[]{:S(2)}, u32[]{:S(2)}) collective-permute-start(bf16[1024,768]{0,1:T(8,128)(2,1)} %get-tuple-element.62), channel_id=1, source_target_pairs={{0,4},{4,0},{8,12},{12,8},{16,20},{20,16},{24,28},{28,24},{1,5},{5... | collective-permute-start | bytes 4718600 | tf_op jit(solution)/shard_map/ppermute | solution.py:445
  534.7 99.9 %collective-permute-start.7 = (bf16[1024,768]{0,1:T(8,128)(2,1)}, bf16[1024,768]{0,1:T(8,128)(2,1)}, u32[]{:S(2)}, u32[]{:S(2)}) collective-permute-start(bf16[1024,768]{0,1:T(8,128)(2,1)} %get-tuple-element.64), channel_id=1, source_target_pairs={{0,8},{4,12},{8,0},{12,4},{16,24},{20,28},{24,16},{28,20},{1,9},{5... | collective-permute-start | bytes 4718600 | tf_op jit(solution)/shard_map/ppermute | solution.py:445
  535.0 99.6 %collective-permute-start.8 = (bf16[1024,768]{0,1:T(8,128)(2,1)}, bf16[1024,768]{0,1:T(8,128)(2,1)}, u32[]{:S(2)}, u32[]{:S(2)}) collective-permute-start(bf16[1024,768]{0,1:T(8,128)(2,1)} %get-tuple-element.63), channel_id=1, source_target_pairs={{0,12},{4,8},{8,4},{12,0},{16,28},{20,24},{24,20},{28,16},{1,13},{... | collective-permute-start | bytes 4718600 | tf_op jit(solution)/shard_map/ppermute | solution.py:445
  (36 other events, 157.0 us)
Sparse Core Ops, SparseCore 0:
  11.6 119.1 all-gather.2
  411.5 135.9 reduce-scatter.1
